TPU v7x, 128 devices: a whole 4x4x4 slice. The times are simulated.
128 devices in a mesh: row: 8 (over x, y_lo), col: 16 (over y_hi, z, core).
Axes of the slice: x: 4, y: 4 (y_hi: 2, y_lo: 2; y = y_hi * 2 + y_lo), z: 4, core: 2. Of those that a mesh axis runs over, the one named last changes fastest.
Arguments:
- multiplier: float32 [512, 20480], P(('row', 'col')), may hold values from -6 to 6
- cycle_tiles: float32 [20480, 512], P('row', 'col'), may hold values from -0.0625 to 0.0625
Outputs:
- symmetric: float32 [512, 512], P(('row', 'col'))
All inputs are finite; a program needn't handle non-finite values.
Results may differ from a plain program's by a relative error of at most 0.00007.
Values sent between devices are 32-bit elements; how exact they have to be, the bound alone decides.
No kernel may reach another device: no remote copies, remote signals or barrier semaphores. Data moves between devices by JAX's collectives and lax.ppermute only.
A program may use at most 64 MiB of HBM per device.

v0:
```python
import jax
import jax.numpy as jnp
from jax import lax
from jax.sharding import PartitionSpec as P

O = 40
V = 512
OW = 1


def on_device(multiplier, cycle_tiles):
    rows_loc, full_width = multiplier.shape
    row_count = lax.axis_size("row")
    col_count = lax.axis_size("col")
    devices = row_count * col_count
    block_width = full_width // devices
    out_block = cycle_tiles.shape[1] // row_count
    virt_dev = rows_loc // OW
    all_rows = rows_loc * devices
    pieces = multiplier.reshape(1, rows_loc, devices, block_width)
    moved = lax.all_to_all(pieces, ("row", "col"), split_axis=2, concat_axis=0, tiled=True)
    direct = moved.reshape(all_rows, block_width)
    swapped = jnp.transpose(multiplier.reshape(virt_dev, OW, V, O), (2, 1, 0, 3)).reshape(
        all_rows, block_width
    )
    combined = 2.0 * direct - swapped
    partial_value = jnp.dot(
        lax.all_gather(combined, "col", axis=1, tiled=True),
        cycle_tiles,
        precision=lax.Precision.HIGHEST,
        preferred_element_type=jnp.float32,
    )
    partial_value = partial_value.reshape(all_rows, row_count, out_block)
    summed = lax.psum_scatter(partial_value, "row", scatter_dimension=1, tiled=True)
    own_cols = summed.reshape(all_rows, out_block)
    outgoing = own_cols.reshape(devices, rows_loc, 1, out_block)
    arrived = lax.all_to_all(outgoing, ("row", "col"), split_axis=0, concat_axis=2, tiled=True)
    own_rows = arrived.reshape(rows_loc, devices * out_block)
    mirrored = jnp.transpose(own_cols.reshape(V, OW, virt_dev, OW), (2, 1, 0, 3)).reshape(
        rows_loc, devices * out_block
    )
    return own_rows + mirrored


def solution(mesh):
    placed = (P(("row", "col"), None), P("row", "col"))
    return jax.shard_map(
        on_device, mesh=mesh, in_specs=placed, out_specs=P(("row", "col"), None), check_vma=False
    )
```

profile of v0, /device:TPU:1, one launch (start us, length us, event | category | flops | bytes accessed | tf_op | source)
XLA Modules:
  0.0 197.9 jit_solution(7017559287507484059)
XLA Ops:
  6.5 0.0 copy-start
  6.5 1.3 reshape.25
  7.9 1.1 copy.14
  9.0 11.5 %all-to-all-start = ((f32[1,4,128,160]{3,1,0,2:T(4,128)}), f32[1,4,128,160]{3,1,0,2:T(4,128)S(1)}, u32[]{:S(2)}, u32[]{:S(2)}) async-start(f32[1,4,128,160]{3,1,0,2:T(4,128)} %copy.14), calls=%async_computation | async-start | bytes 1048576 | tf_op jit(solution)/shard_map/all_to_all | solution.py:21
  20.5 0.0 all-gather.2.cloned.1.call-start
  20.6 1.8 reshape.26
  22.4 0.3 copy.15
  22.7 0.0 copy-start.1
  22.7 11.6 %all-to-all-done = f32[1,4,128,160]{3,1,0,2:T(4,128)S(1)} async-done(((f32[1,4,128,160]{3,1,0,2:T(4,128)}), f32[1,4,128,160]{3,1,0,2:T(4,128)S(1)}, u32[]{:S(2)}, u32[]{:S(2)}) %all-to-all-start) | async-done | bytes 327712 | tf_op jit(solution)/shard_map/all_to_all | solution.py:21
  34.3 0.1 multiply_bitcast_fusion
  34.4 0.2 mul.19
  34.6 0.2 copy.16
  34.8 0.8 bitcast_subtract_fusion
  35.5 0.0 all-gather.2.cloned.1.call-update
  35.6 0.0 all-reduce.3.cloned.1.call-start
  35.6 55.7 %all-gather.2.cloned.1.call-done = f32[512,2560]{0,1:T(8,128)} async-done(((f32[512,160]{0,1:T(8,128)}), f32[512,2560]{0,1:T(8,128)}) %all-gather.2.cloned.1.call-update) | async-done | bytes 5242896 | tf_op jit(solution)/shard_map/all_gather | solution.py:28
  91.3 0.0 copy-done
  91.3 5.7 %fusion = f32[512,32]{0,1:T(8,128)S(1)} fusion(f32[512,2560]{0,1:T(8,128)} %all-gather.2.cloned.1.call-done, f32[2560,32]{0,1:T(8,128)S(1)} %copy-done), kind=kOutput, calls=%fused_computation.4 | convolution fusion | flops 503316480 | bytes 5636096 | tf_op jit(solution)/shard_map/dot_general | solution.py:27
  97.0 0.6 reshape.28
  97.6 0.0 all-reduce.3.cloned.1.call-update
  97.7 0.0 copy-done.1
  97.7 0.6 dynamic-slice
  98.3 65.1 %all-reduce.3.cloned.1.call-done = f32[512,8,4]{0,2,1:T(4,128)} async-done(((f32[512,8,4]{0,2,1:T(4,128)}), f32[512,8,4]{0,2,1:T(4,128)}) %all-reduce.3.cloned.1.call-update) | async-done | bytes 65552
  163.4 1.3 constant_dynamic-slice_fusion
  164.8 0.3 reshape_reshape.6
  165.0 0.2 copy.17
  165.2 23.8 %all_to_all.24 = f32[128,4,1,4]{1,3,2,0:T(4,128)S(1)} all-to-all(f32[128,4,1,4]{1,3,2,0:T(4,128)S(1)} %copy.17), channel_id=1, replica_groups=mesh['row'=8,'col'=16] {'row','col'}, dimensions={0} | all-to-all | bytes 16384 | tf_op jit(solution)/shard_map/all_to_all | solution.py:37
  189.0 0.1 copy.19
  189.1 1.9 bitcast_add_fusion
Async XLA Ops:
  6.5 84.8 %copy-start = (f32[2560,32]{0,1:T(8,128)S(1)}, f32[2560,32]{0,1:T(8,128)}, u32[]{:S(2)}) copy-start(f32[2560,32]{0,1:T(8,128)} %param.3) | copy-start | bytes 983044
  9.0 25.3 %all-to-all-start = ((f32[1,4,128,160]{3,1,0,2:T(4,128)}), f32[1,4,128,160]{3,1,0,2:T(4,128)S(1)}, u32[]{:S(2)}, u32[]{:S(2)}) async-start(f32[1,4,128,160]{3,1,0,2:T(4,128)} %copy.14), calls=%async_computation | async-start | bytes 1048576 | tf_op jit(solution)/shard_map/all_to_all | solution.py:21
  20.5 70.8 %all-gather.2.cloned.1.call-start = ((), (), s32[]{:S(2)}) async-start(), calls=%async_computation.2 | async-start | bytes 5570560 | tf_op jit(solution)/shard_map/all_gather | solution.py:28
  22.7 74.9 %copy-start.1 = (u32[128]{0:T(128)S(1)}, u32[128]{0:T(128)}, u32[]{:S(2)}) copy-start(u32[128]{0:T(128)} %constant.5) | copy-start | bytes 1540
  35.6 127.9 %all-reduce.3.cloned.1.call-start = ((), (), s32[]{:S(2)}) async-start(), calls=%async_computation.3 | async-start | bytes 131072
Sparse Core Ops, SparseCore 0:
  35.7 55.5 all-gather.1
  97.8 65.6 all-reduce.2
where the time goes:
time: 198 us
  waiting for transfers between devices  132 us (67%)
  blocking collectives  23.8 us (12%)
  between operations  13.5 us (7%)
  starting transfers between devices  11.6 us (6%)
  local copies, waits for them, and re-layouts  8.11 us (4%)
  matrix products  5.65 us (3%)
  other arithmetic  2.83 us (1%)
    unnamed x3, waiting for transfers between devices  65.2 us
    all_gather x1, waiting for transfers between devices, on_device(): lax.all_gather(combined, 'col', axis=1, tiled=True)  55.7 us
    all_to_all x1, blocking collectives, on_device(): lax.all_to_all(outgoing, ('row', 'col'), split_axis=0, concat_axis=2, til...  23.8 us
    all_to_all x1, waiting for transfers between devices, on_device(): lax.all_to_all(pieces, ('row', 'col'), split_axis=2, concat_axis=0, tiled...  11.6 us
    all_to_all x1, starting transfers between devices, on_device(): lax.all_to_all(pieces, ('row', 'col'), split_axis=2, concat_axis=0, tiled...  11.5 us
    dot_general x1, matrix products, on_device(): jnp.dot(lax.all_gather(combined, 'col', axis=1, tiled=True), cycle_tiles,...  5.65 us
  transfers between devices with their start and end apart: 3, of which 3 were waited for; matrix products, arithmetic and copies ran while one was open for 1% of the time, Pallas kernels for 0%

commit v1 on v0

v1 whole, which is shorter than its diff:
```python
import jax
import jax.numpy as jnp
from jax import lax
from jax.experimental import pallas as pl
from jax.experimental.pallas import tpu as pltpu
from jax.sharding import PartitionSpec as P

O = 40
V = 512
LANES = 128
PER = 4
DEPTH = PER * O
REST = DEPTH - LANES
DEVICES = V // PER
ROWS_OUT = PER * V // LANES

VMEM = pltpu.VMEM
F32 = jnp.float32


def call(body, out_shapes, scratch=(), flops=0, moved=1 << 20):
    several = isinstance(out_shapes, list)
    outs = [jax.ShapeDtypeStruct(s, F32) for s in (out_shapes if several else [out_shapes])]
    return pl.pallas_call(
        body,
        out_shape=outs if several else outs[0],
        scratch_shapes=list(scratch),
        cost_estimate=pl.CostEstimate(flops=flops, bytes_accessed=moved, transcendentals=0),
        compiler_params=pltpu.CompilerParams(vmem_limit_bytes=16 << 20),
    )


def lane_index(rows):
    return lax.broadcasted_iota(jnp.int32, (rows, LANES), 1)


def rolled(x, shift):
    shift %= LANES
    return x if shift == 0 else pltpu.roll(x, shift, 1)


def window(parts, start, rows):
    first, off = divmod(start, LANES)
    if off == 0:
        return parts(first)
    low, high = rolled(parts(first), -off), rolled(parts(first + 1), -off)
    return jnp.where(lane_index(rows) < LANES - off, low, high)


def pack_multiplier(m_ref, out_ref):
    groups = DEVICES // 4
    lane = lane_index(groups)
    for j in range(4):
        rest = None
        for i in range(PER):
            piece = lambda n, i=i: m_ref[pl.ds(4 * n + i, groups, stride=20), :]
            out_ref[pl.ds(5 * j + i, groups, stride=20), :] = window(piece, DEPTH * j, groups)
            tail = rolled(piece(j + 1), REST * (i - j))
            rest = tail if rest is None else jnp.where(lane >= REST * i, tail, rest)
        out_ref[pl.ds(5 * j + 4, groups, stride=20), :] = rest


def pack_swapped(m_ref, out_ref):
    groups = DEVICES // 4
    lane = lane_index(groups)
    for j in range(4):
        rest = None
        for i in range(PER):
            u = 4 * j + i
            main = None
            for c in range(PER):
                piece = lambda n, c=c: m_ref[pl.ds(4 * n + c, groups, stride=20), :]
                first, off = divmod(O * u, LANES)
                block = piece(first)
                if off + O > LANES:
                    block = jnp.where(lane >= off, block, piece(first + 1))
                at = O * c
                block_main = rolled(block, at - off)
                main = block_main if main is None else jnp.where(lane >= at, block_main, main)
                if at + O > LANES:
                    keep = LANES - at
                    tail = rolled(block, REST * i - off - keep)
                    rest = tail if rest is None else jnp.where(lane >= REST * i, tail, rest)
            out_ref[pl.ds(5 * j + i, groups, stride=20), :] = main
        out_ref[pl.ds(5 * j + 4, groups, stride=20), :] = rest


def pack_cycle(w_ref, out_ref):
    cols = w_ref.shape[0]
    count = w_ref.shape[1] // DEPTH
    lane = lane_index(8)
    for e in range(count):
        rest = None
        for g in range(cols // 8):
            piece = lambda n, g=g: w_ref[8 * g : 8 * g + 8, LANES * n : LANES * n + LANES]
            out_ref[40 * e + 8 * g : 40 * e + 8 * g + 8, :] = window(piece, DEPTH * e, 8)
            first, off = divmod(DEPTH * e + LANES, LANES)
            tail = rolled(piece(first), REST * g - off)
            rest = tail if rest is None else jnp.where(lane >= REST * g, tail, rest)
        out_ref[40 * e + 32 : 40 * e + 40, :] = rest


def update(got_ref, swapped_ref, w_ref, out_ref, x_ref, p_ref, pr_ref, q_ref, qr_ref):
    lane = lane_index(DEVICES)
    x_ref[...] = 2.0 * got_ref[...] - swapped_ref[...]
    packed = x_ref[pl.ds(4, DEVICES, stride=5), :]
    n_col = w_ref.shape[0] // 40
    n_row = DEVICES // n_col
    for i in range(PER):
        a_main = x_ref[pl.ds(i, DEVICES, stride=5), :]
        a_rest = rolled(packed, -REST * i)
        w_main = jnp.concatenate(
            [w_ref[pl.ds(4 * r + i, n_col, stride=40), :] for r in range(n_row)], axis=0
        )
        w_rest = jnp.concatenate(
            [
                rolled(w_ref[pl.ds(32 + 4 * (r % 2) + i, n_col, stride=40), :], REST * (1 - r // 2))
                for r in range(n_row)
            ],
            axis=0,
        )
        rows = slice(DEVICES * i, DEVICES * i + DEVICES)
        spread = pl.ds(i, DEVICES, stride=4)
        p_ref[rows, :LANES] = a_main
        p_ref[rows, LANES:] = w_main
        q_ref[0, spread, :] = w_main
        q_ref[1, spread, :] = a_main
        pr_ref[rows, :] = jnp.where(lane < REST, a_rest, jnp.where(lane < 2 * REST, w_rest, 0.0))
        w_first, a_second = rolled(w_rest, -REST), rolled(a_rest, REST)
        qr_ref[spread, :] = jnp.where(lane < REST, w_first, jnp.where(lane < 2 * REST, a_second, 0.0))

    def product(x, y):
        return lax.dot_general(
            x, y, (((1,), (1,)), ((), ())), precision=lax.Precision.HIGHEST, preferred_element_type=F32
        )

    for i in range(PER):
        rows = slice(DEVICES * i, DEVICES * i + DEVICES)
        term = product(p_ref[rows, :LANES], q_ref[0])
        term += product(p_ref[rows, LANES:], q_ref[1])
        term += product(pr_ref[rows, :], qr_ref[...])
        for m in range(V // LANES):
            out_ref[pl.ds(4 * m + i, DEVICES, stride=ROWS_OUT), :] = term[:, LANES * m : LANES * m + LANES]


def finish(parts_ref, out_ref):
    total = parts_ref[0:ROWS_OUT, :]
    for n in range(1, parts_ref.shape[0] // ROWS_OUT):
        total += parts_ref[ROWS_OUT * n : ROWS_OUT * n + ROWS_OUT, :]
    for m in range(V // LANES):
        out_ref[:, LANES * m : LANES * m + LANES] = total[4 * m : 4 * m + 4, :]


def on_device(multiplier, cycle_tiles):
    n_col = lax.axis_size("col")
    both = ("row", "col")
    slab = multiplier.reshape(PER, DEPTH, LANES).transpose(1, 0, 2).reshape(PER * DEPTH, LANES)
    cycle_rows = cycle_tiles.T
    packed = call(pack_multiplier, (5 * DEVICES, LANES))(slab)
    got = lax.all_to_all(packed.reshape(DEVICES, 1, 5 * LANES), both, 0, 0, tiled=True)
    w_packed = call(pack_cycle, (40 * n_col, LANES))(cycle_rows)
    w_got = lax.all_to_all(w_packed.reshape(n_col, 40, LANES), "col", 0, 0, tiled=True)
    swapped = call(pack_swapped, (5 * DEVICES, LANES))(slab)
    share = call(
        update,
        (ROWS_OUT * DEVICES, LANES),
        scratch=[
            VMEM((5 * DEVICES, LANES), F32),
            VMEM((V, 2 * LANES), F32),
            VMEM((V, LANES), F32),
            VMEM((2, V, LANES), F32),
            VMEM((V, LANES), F32),
        ],
        flops=2 * V * V * 2 * DEPTH * 6,
    )(got.reshape(5 * DEVICES, LANES), swapped, w_got.reshape(40 * n_col, LANES))
    parts = lax.all_to_all(share.reshape(DEVICES, ROWS_OUT, LANES), both, 0, 0, tiled=True)
    return call(finish, (PER, V))(parts.reshape(DEVICES * ROWS_OUT, LANES))


def solution(mesh):
    placed = (P(("row", "col"), None), P("row", "col"))
    return jax.shard_map(
        on_device, mesh=mesh, in_specs=placed, out_specs=P(("row", "col"), None), check_vma=False
    )
```

time: 198 us -> 65.3 us (0.33)
  waiting for transfers between devices: 132 us -> 19.8 us
  between operations: 13.5 us -> 0.03 us
  local copies, waits for them, and re-layouts: 8.11 us -> 0.98 us
  Pallas kernels: 0 us -> 5.97 us
  matrix products: 5.65 us -> 0 us
  starting transfers between devices: 11.6 us -> 15.4 us
  other arithmetic: 2.83 us -> 0 us
    unnamed x3 -> x0, waiting for transfers between devices: 65.2 us -> none
    all_gather x1 -> x0, waiting for transfers between devices: 55.7 us -> none  [on_device(): lax.all_gather(combined, 'col', axis=1, tiled=True)]
    all_to_all x1 -> x2, waiting for transfers between devices: 11.6 us -> 19.8 us  [the longest x1 11.6 us: on_device(): lax.all_to_all(packed.reshape(DEVICES, 1, 5 * LANES), both, 0, 0, tiled=T...]
    pallas_call x0 -> x5, Pallas kernels: none -> 5.97 us  [the longest x1 2.98 us: on_device(): call(update, (ROWS_OUT * DEVICES, LANES), scratch=[VMEM((5 * DEVICES, LAN...]
    dot_general x1 -> x0, matrix products: 5.65 us -> none  [on_device(): jnp.dot(lax.all_gather(combined, 'col', axis=1, tiled=True), cycle_tiles,...]
    reshape x5 -> x0, local copies, waits for them, and re-layouts: 5.05 us -> none  [the longest x2 2.48 us: on_device(): pieces = multiplier.reshape(1, rows_loc, devices, block_width)]
    all_to_all x1 -> x2, starting transfers between devices: 11.5 us -> 15.4 us  [the longest x1 9.58 us: on_device(): lax.all_to_all(w_packed.reshape(n_col, 40, LANES), 'col', 0, 0, tiled=True)]
  transfers between devices with their start and end apart: 3 -> 2, of which waited for: 3 -> 2; matrix products, arithmetic and copies ran while one was open for 1% -> 0% of each run, Pallas kernels for 0% -> 2%
where the time goes in v1:
time: 65.3 us; the launch traced here: 65 us
  blocking collectives  22.8 us (35%)
  waiting for transfers between devices  19.8 us (30%)
  starting transfers between devices  15.4 us (24%)
  Pallas kernels  5.97 us (9%)
  local copies, waits for them, and re-layouts  0.98 us (2%)
    all_to_all x1, blocking collectives, on_device(): lax.all_to_all(share.reshape(DEVICES, ROWS_OUT, LANES), both, 0, 0, tiled...  22.8 us
    all_to_all x1, waiting for transfers between devices, on_device(): lax.all_to_all(packed.reshape(DEVICES, 1, 5 * LANES), both, 0, 0, tiled=T...  11.6 us
    all_to_all x1, starting transfers between devices, on_device(): lax.all_to_all(w_packed.reshape(n_col, 40, LANES), 'col', 0, 0, tiled=True)  9.58 us
    all_to_all x1, waiting for transfers between devices, on_device(): lax.all_to_all(w_packed.reshape(n_col, 40, LANES), 'col', 0, 0, tiled=True)  8.23 us
    all_to_all x1, starting transfers between devices, on_device(): lax.all_to_all(packed.reshape(DEVICES, 1, 5 * LANES), both, 0, 0, tiled=T...  5.79 us
    pallas_call x1, Pallas kernels, on_device(): call(update, (ROWS_OUT * DEVICES, LANES), scratch=[VMEM((5 * DEVICES, LAN...  2.98 us
  transfers between devices with their start and end apart: 2, of which 2 were waited for; matrix products, arithmetic and copies ran while one was open for 0% of the time, Pallas kernels for 2%

profile of v1, /device:TPU:1, one launch (start us, length us, event | category | flops | bytes accessed | tf_op | source)
XLA Modules:
  0.0 65.0 jit_solution(6679504548653574585)
XLA Ops:
  0.0 0.0 copy-start.1
  0.0 1.0 %copy-done.1 = f32[2560,32]{0,1:T(8,128)S(1)} copy-done((f32[2560,32]{0,1:T(8,128)S(1)}, f32[2560,32]{0,1:T(8,128)}, u32[]{:S(2)}) %copy-start.1) | copy-done | bytes 327704
  1.0 0.9 %shard_map.30 = f32[640,128]{1,0:T(8,128)} custom-call(f32[32,2560]{1,0:T(8,128)S(1)} %bitcast.16), custom_call_target="tpu_custom_call" | custom-call | bytes 1048576 | tf_op jit(solution)/shard_map/pallas_call | solution.py:161
  1.9 0.0 copy-start
  1.9 9.6 %all-to-all-start.1 = ((f32[16,40,128]{2,1,0:T(8,128)}), f32[16,40,128]{2,1,0:T(8,128)S(1)}, u32[]{:S(2)}, u32[]{:S(2)}) async-start(f32[16,40,128]{2,1,0:T(8,128)} %bitcast.8), calls=%async_computation.1 | async-start | bytes 655360 | tf_op jit(solution)/shard_map/all_to_all | solution.py:162
  11.5 0.0 copy-done
  11.5 0.9 %shard_map.28 = f32[640,128]{1,0:T(8,128)} custom-call(f32[640,128]{1,0:T(8,128)S(1)} %bitcast.13), custom_call_target="tpu_custom_call" | custom-call | bytes 1048576 | tf_op jit(solution)/shard_map/pallas_call | solution.py:159
  12.4 8.2 %all-to-all-done.1 = f32[16,40,128]{2,1,0:T(8,128)S(1)} async-done(((f32[16,40,128]{2,1,0:T(8,128)}), f32[16,40,128]{2,1,0:T(8,128)S(1)}, u32[]{:S(2)}, u32[]{:S(2)}) %all-to-all-start.1) | async-done | bytes 327712 | tf_op jit(solution)/shard_map/all_to_all | solution.py:162
  20.7 5.8 %all-to-all-start = ((f32[128,1,640]{2,1,0:T(1,128)}), f32[128,1,640]{2,1,0:T(1,128)S(1)}, u32[]{:S(2)}, u32[]{:S(2)}) async-start(f32[128,1,640]{2,1,0:T(1,128)} %bitcast.3), calls=%async_computation | async-start | bytes 655360 | tf_op jit(solution)/shard_map/all_to_all | solution.py:160
  26.5 0.4 shard_map.29.swapped_ref
  26.8 11.6 %all-to-all-done = f32[128,1,640]{2,1,0:T(1,128)S(1)} async-done(((f32[128,1,640]{2,1,0:T(1,128)}), f32[128,1,640]{2,1,0:T(1,128)S(1)}, u32[]{:S(2)}, u32[]{:S(2)}) %all-to-all-start) | async-done | bytes 327712 | tf_op jit(solution)/shard_map/all_to_all | solution.py:160
  38.4 3.0 %shard_map.31 = f32[2048,128]{1,0:T(8,128)S(1)} custom-call(f32[640,128]{1,0:T(8,128)S(1)} %bitcast.18, f32[640,128]{1,0:T(8,128)S(1)} %shard_map.29.swapped_ref, f32[640,128]{1,0:T(8,128)S(1)} %bitcast.17), custom_call_target="tpu_custom_call" | custom-call | flops 1006632960 | bytes 1048576 | tf_op jit(solution)/shard_map/pallas_call | solution.py:164
  41.4 22.8 %all_to_all.15 = f32[128,16,128]{2,1,0:T(8,128)S(1)} all-to-all(f32[128,16,128]{2,1,0:T(8,128)S(1)} %bitcast.15), channel_id=1, replica_groups=mesh['row'=8,'col'=16] {'row','col'}, dimensions={0} | all-to-all | bytes 2097152 | tf_op jit(solution)/shard_map/all_to_all | solution.py:176
  64.2 0.7 %shard_map.32 = f32[4,512]{1,0:T(4,128)} custom-call(f32[2048,128]{1,0:T(8,128)S(1)} %bitcast.12), custom_call_target="tpu_custom_call" | custom-call | bytes 1048576 | tf_op jit(solution)/shard_map/pallas_call | solution.py:177
Async XLA Ops:
  0.0 1.0 %copy-start.1 = (f32[2560,32]{0,1:T(8,128)S(1)}, f32[2560,32]{0,1:T(8,128)}, u32[]{:S(2)}) copy-start(f32[2560,32]{0,1:T(8,128)} %param.3) | copy-start | bytes 983044
  1.9 9.6 %copy-start = (f32[4,20480]{1,0:T(4,128)S(1)}, f32[4,20480]{1,0:T(4,128)}, u32[]{:S(2)}) copy-start(f32[4,20480]{1,0:T(4,128)} %param.2) | copy-start | bytes 983044
  1.9 18.8 %all-to-all-start.1 = ((f32[16,40,128]{2,1,0:T(8,128)}), f32[16,40,128]{2,1,0:T(8,128)S(1)}, u32[]{:S(2)}, u32[]{:S(2)}) async-start(f32[16,40,128]{2,1,0:T(8,128)} %bitcast.8), calls=%async_computation.1 | async-start | bytes 655360 | tf_op jit(solution)/shard_map/all_to_all | solution.py:162
  20.7 17.7 %all-to-all-start = ((f32[128,1,640]{2,1,0:T(1,128)}), f32[128,1,640]{2,1,0:T(1,128)S(1)}, u32[]{:S(2)}, u32[]{:S(2)}) async-start(f32[128,1,640]{2,1,0:T(1,128)} %bitcast.3), calls=%async_computation | async-start | bytes 655360 | tf_op jit(solution)/shard_map/all_to_all | solution.py:160

commit v2 on v1

v2 whole, which is shorter than its diff:
```python
import jax
import jax.numpy as jnp
from jax import lax
from jax.experimental import pallas as pl
from jax.experimental.pallas import tpu as pltpu
from jax.sharding import Mesh, PartitionSpec as P

O = 40
V = 512
LANES = 128
PER = 4
DEPTH = PER * O
REST = DEPTH - LANES
DEVICES = V // PER
CHIPS = DEVICES // 2
ROWS_OUT = PER * V // LANES
CHUNK = 40
N_YZ = 8
FAR = (0, 4)

VMEM = pltpu.VMEM
F32 = jnp.float32


def call(body, out_shapes, scratch=(), flops=0, moved=1 << 20):
    several = isinstance(out_shapes, list)
    outs = [jax.ShapeDtypeStruct(s, F32) for s in (out_shapes if several else [out_shapes])]
    return pl.pallas_call(
        body,
        out_shape=outs if several else outs[0],
        scratch_shapes=list(scratch),
        cost_estimate=pl.CostEstimate(flops=flops, bytes_accessed=moved, transcendentals=0),
        compiler_params=pltpu.CompilerParams(vmem_limit_bytes=16 << 20),
    )


def lane_index(rows):
    return lax.broadcasted_iota(jnp.int32, (rows, LANES), 1)


def rolled(x, shift):
    shift %= LANES
    return x if shift == 0 else pltpu.roll(x, shift, 1)


def window(parts, start, rows):
    first, off = divmod(start, LANES)
    if off == 0:
        return parts(first)
    low, high = rolled(parts(first), -off), rolled(parts(first + 1), -off)
    return jnp.where(lane_index(rows) < LANES - off, low, high)


def chunk(n):
    return pl.ds(CHUNK * n if isinstance(n, int) else pl.multiple_of(CHUNK * n, 8), CHUNK)


def pack_multiplier(m_ref, out_ref):
    groups = DEVICES // 4
    lane = lane_index(groups)
    for j in range(4):
        rest = None
        for i in range(PER):
            piece = lambda n, i=i: m_ref[pl.ds(4 * n + i, groups, stride=20), :]
            out_ref[pl.ds(5 * j + i, groups, stride=20), :] = window(piece, DEPTH * j, groups)
            tail = rolled(piece(j + 1), REST * (i - j))
            rest = tail if rest is None else jnp.where(lane >= REST * i, tail, rest)
        out_ref[pl.ds(5 * j + 4, groups, stride=20), :] = rest


def pack_swapped(m_ref, out_ref):
    groups = DEVICES // 4
    lane = lane_index(groups)
    for j in range(4):
        rest = None
        for i in range(PER):
            u = 4 * j + i
            main = None
            for c in range(PER):
                piece = lambda n, c=c: m_ref[pl.ds(4 * n + c, groups, stride=20), :]
                first, off = divmod(O * u, LANES)
                block = piece(first)
                if off + O > LANES:
                    block = jnp.where(lane >= off, block, piece(first + 1))
                at = O * c
                block_main = rolled(block, at - off)
                main = block_main if main is None else jnp.where(lane >= at, block_main, main)
                if at + O > LANES:
                    keep = LANES - at
                    tail = rolled(block, REST * i - off - keep)
                    rest = tail if rest is None else jnp.where(lane >= REST * i, tail, rest)
            out_ref[pl.ds(5 * j + i, groups, stride=20), :] = main
        out_ref[pl.ds(5 * j + 4, groups, stride=20), :] = rest


def pack_cycle(w_ref, own_ref, other_ref, all_ref):
    lane = lane_index(8)
    for e in range(2 * N_YZ):
        rest = None
        for g in range(PER):
            piece = lambda n, g=g: w_ref[8 * g : 8 * g + 8, LANES * n : LANES * n + LANES]
            all_ref[CHUNK * e + 8 * g : CHUNK * e + 8 * g + 8, :] = window(piece, DEPTH * e, 8)
            first, off = divmod(DEPTH * e + LANES, LANES)
            tail = rolled(piece(first), REST * g - off)
            rest = tail if rest is None else jnp.where(lane >= REST * g, tail, rest)
        all_ref[CHUNK * e + 32 : CHUNK * e + 40, :] = rest
    core = lax.axis_index("core")
    for yz in range(N_YZ):
        own_ref[chunk(yz), :] = all_ref[chunk(2 * yz + core), :]
        other_ref[chunk(yz), :] = all_ref[chunk(2 * yz + 1 - core), :]


def turn_far(own_ref, other_ref, *out_refs):
    me = lax.axis_index("yz")
    for k, ref in zip(FAR, out_refs):
        for z in range(4):
            for s, came in enumerate((own_ref, other_ref)):
                ref[chunk(2 * z + s), :] = came[chunk(((me ^ k) & 4) + z), :]


def turn_near(*refs):
    came, out_refs = refs[: len(FAR)], refs[len(FAR) :]
    z = lax.axis_index("yz") & 3
    for j, ref in enumerate(out_refs):
        for n, piece in enumerate(came):
            for s in range(2):
                ref[chunk(2 * n + s), :] = piece[chunk(2 * (z ^ j) + s), :]


def product(x, y):
    return lax.dot_general(
        x, y, (((1,), (1,)), ((), ())), precision=lax.Precision.HIGHEST, preferred_element_type=F32
    )


def half_update(p_ref, q_ref, out_ref):
    term = product(p_ref[...], jnp.concatenate([q_ref[n] for n in range(3)], axis=1))
    for i in range(PER):
        for m in range(V // LANES):
            piece = term[CHIPS * i : CHIPS * i + CHIPS, LANES * m : LANES * m + LANES]
            out_ref[pl.ds(4 * m + i, CHIPS, stride=ROWS_OUT), :] = piece


def first_half(got_ref, swapped_ref, w0, w1, w2, w3, out_ref, p_own, q_ref, x_ref, w_ref, p_ref):
    me, core = lax.axis_index("yz"), lax.axis_index("core")
    for j, ref in enumerate((w0, w1, w2, w3)):
        for n, k in enumerate(FAR):
            for s in range(2):
                w_ref[chunk(2 * (me ^ k ^ j) + (core ^ s)), :] = ref[chunk(2 * n + s), :]
    x_ref[...] = 2.0 * got_ref[...] - swapped_ref[...]
    lane = lane_index(CHIPS)
    n_row = DEVICES // (2 * N_YZ)
    for parity, p_out in ((1 - core, p_ref), (core, p_own)):
        packed = x_ref[pl.ds(5 * parity + 4, CHIPS, stride=10), :]
        for i in range(PER):
            a_main = x_ref[pl.ds(5 * parity + i, CHIPS, stride=10), :]
            a_rest = rolled(packed, -REST * i)
            w_main = jnp.concatenate(
                [w_ref[pl.ds(CHUNK * parity + 4 * r + i, N_YZ, stride=2 * CHUNK), :] for r in range(n_row)], axis=0
            )
            w_rest = jnp.concatenate(
                [
                    rolled(
                        w_ref[pl.ds(CHUNK * parity + 32 + 4 * (r % 2) + i, N_YZ, stride=2 * CHUNK), :],
                        REST * (1 - r // 2),
                    )
                    for r in range(n_row)
                ],
                axis=0,
            )
            rows = slice(CHIPS * i, CHIPS * i + CHIPS)
            spread = pl.ds(4 * parity + i, CHIPS, stride=8)
            p_out[rows, :LANES] = a_main
            p_out[rows, LANES : 2 * LANES] = w_main
            q_ref[0, spread, :] = w_main
            q_ref[1, spread, :] = a_main
            p_out[rows, 2 * LANES :] = jnp.where(lane < REST, a_rest, jnp.where(lane < 2 * REST, w_rest, 0.0))
            w_first, a_second = rolled(w_rest, -REST), rolled(a_rest, REST)
            q_ref[2, spread, :] = jnp.where(
                lane < REST, w_first, jnp.where(lane < 2 * REST, a_second, 0.0)
            )
    half_update(p_ref, q_ref, out_ref)


def finish(parts_ref, out_ref):
    total = parts_ref[0:ROWS_OUT, :]
    for n in range(1, parts_ref.shape[0] // ROWS_OUT):
        total += parts_ref[ROWS_OUT * n : ROWS_OUT * n + ROWS_OUT, :]
    for m in range(V // LANES):
        out_ref[:, LANES * m : LANES * m + LANES] = total[4 * m : 4 * m + 4, :]


def swap(x, axis, k):
    return lax.ppermute(x, axis, [(n, n ^ k) for n in range(lax.axis_size(axis))])


def on_device(multiplier, cycle_tiles):
    slab = multiplier.reshape(PER, DEPTH, LANES).transpose(1, 0, 2).reshape(PER * DEPTH, LANES)
    half, quarter = (N_YZ * CHUNK, LANES), (4 * CHUNK, LANES)
    own, other = call(pack_cycle, [half] * 2, scratch=[VMEM((2 * N_YZ * CHUNK, LANES), F32)])(cycle_tiles.T)
    other = swap(other, "core", 1)
    packed = call(pack_multiplier, (5 * DEVICES, LANES))(slab)
    far = call(turn_far, [half] * 2)(own, other)
    far = [far[0], *(swap(x, "yz", k) for k, x in zip(FAR[1:], far[1:]))]
    got = lax.all_to_all(
        packed.reshape(DEVICES, 1, 5 * LANES), ("row", "yz", "core"), 0, 0, tiled=True
    )
    near = call(turn_near, [quarter] * 4)(*far)
    near = [near[0], *(swap(x, "yz", j) for j, x in enumerate(near) if j)]
    swapped = call(pack_swapped, (5 * DEVICES, LANES))(slab)
    width = 3 * LANES
    rows, flops = CHIPS * ROWS_OUT, V * V * width * 6
    theirs, p_own, q = call(
        first_half,
        [(rows, LANES), (V // 2, width), (3, V, LANES)],
        scratch=[
            VMEM((5 * DEVICES, LANES), F32),
            VMEM((2 * N_YZ * CHUNK, LANES), F32),
            VMEM((V // 2, width), F32),
        ],
        flops=flops,
    )(got.reshape(5 * DEVICES, LANES), swapped, *near)
    theirs = swap(theirs, "core", 1)
    mine = call(half_update, (rows, LANES), flops=flops)(p_own, q)
    share = mine + theirs
    parts = lax.all_to_all(share.reshape(CHIPS, ROWS_OUT, LANES), ("row", "yz"), 0, 0, tiled=True)
    return call(finish, (PER, V))(parts.reshape(rows, LANES))


def solution(mesh):
    n_row = mesh.shape["row"]
    split = Mesh(mesh.devices.reshape(n_row, N_YZ, 2), ("row", "yz", "core"))
    every = ("row", "yz", "core")
    return jax.shard_map(
        on_device,
        mesh=split,
        in_specs=(P(every, None), P("row", ("yz", "core"))),
        out_specs=P(every, None),
        check_vma=False,
    )
```

time: 65.3 us -> 57.7 us (0.88)
  waiting for transfers between devices: 19.8 us -> 12 us
  starting transfers between devices: 15.4 us -> 21.7 us
  blocking collectives: 22.8 us -> 17.2 us
  Pallas kernels: 5.97 us -> 4.87 us
    all_to_all x2 -> x1, waiting for transfers between devices: 19.8 us -> 0.01 us  [on_device(): lax.all_to_all(packed.reshape(DEVICES, 1, 5 * LANES), ('row', 'yz', 'core...]
    ppermute x0 -> x6, waiting for transfers between devices: none -> 12 us  [swap(): lax.ppermute(x, axis, [(n, n ^ k) for n in range(lax.axis_size(axis))])]
    ppermute x0 -> x6, starting transfers between devices: none -> 11.5 us  [swap(): lax.ppermute(x, axis, [(n, n ^ k) for n in range(lax.axis_size(axis))])]
    all_to_all x1, blocking collectives: 22.8 us -> 17.2 us  [on_device(): lax.all_to_all(share.reshape(CHIPS, ROWS_OUT, LANES), ('row', 'yz'), 0, 0...]
    all_to_all x2 -> x1, starting transfers between devices: 15.4 us -> 10.2 us  [on_device(): lax.all_to_all(packed.reshape(DEVICES, 1, 5 * LANES), ('row', 'yz', 'core...]
    pallas_call x3 -> x6, Pallas kernels: 4.67 us -> 3.58 us  [the longest x1 1.45 us: on_device(): call(first_half, [(rows, LANES), (V // 2, width), (3, V, LANES)], scratch...]
  transfers between devices with their start and end apart: 2 -> 7, of which waited for: 2 -> 4; matrix products, arithmetic and copies ran while one was open for 0% -> 0% of each run, Pallas kernels for 2% -> 4%
where the time goes in v2:
time: 57.7 us; the launch traced here: 56.9 us
  starting transfers between devices  21.7 us (38%)
  blocking collectives  17.2 us (30%)
  waiting for transfers between devices  12 us (21%)
  Pallas kernels  4.87 us (8%)
  local copies, waits for them, and re-layouts  1.02 us (2%)
    all_to_all x1, blocking collectives, on_device(): lax.all_to_all(share.reshape(CHIPS, ROWS_OUT, LANES), ('row', 'yz'), 0, 0...  17.2 us
    ppermute x6, waiting for transfers between devices, swap(): lax.ppermute(x, axis, [(n, n ^ k) for n in range(lax.axis_size(axis))])  12 us
    ppermute x6, starting transfers between devices, swap(): lax.ppermute(x, axis, [(n, n ^ k) for n in range(lax.axis_size(axis))])  11.5 us
    all_to_all x1, starting transfers between devices, on_device(): lax.all_to_all(packed.reshape(DEVICES, 1, 5 * LANES), ('row', 'yz', 'core...  10.2 us
    pallas_call x1, Pallas kernels, on_device(): call(first_half, [(rows, LANES), (V // 2, width), (3, V, LANES)], scratch...  1.45 us
  transfers between devices with their start and end apart: 7, of which 4 were waited for; matrix products, arithmetic and copies ran while one was open for 0% of the time, Pallas kernels for 4%

profile of v2, /device:TPU:1, one launch (start us, length us, event | category | flops | bytes accessed | tf_op | source)
XLA Modules:
  0.0 56.9 jit_solution(3975734233985358264)
XLA Ops:
  0.0 0.0 copy-start
  0.0 0.0 copy-start.1
  0.0 1.0 %copy-done.1 = f32[2560,32]{0,1:T(8,128)S(1)} copy-done((f32[2560,32]{0,1:T(8,128)S(1)}, f32[2560,32]{0,1:T(8,128)}, u32[]{:S(2)}) %copy-start.1) | copy-done | bytes 327704
  1.0 0.3 shard_map.30
  1.3 1.4 %collective-permute-start = (f32[320,128]{1,0:T(8,128)S(1)}, f32[320,128]{1,0:T(8,128)S(1)}, u32[]{:S(2)}, u32[]{:S(2)}) collective-permute-start(f32[320,128]{1,0:T(8,128)S(1)} %get-tuple-element.17), channel_id=1, source_target_pairs={{0,1},{1,0},{2,3},{3,2},{4,5},{5,4},{6,7},{7,6},{8,9},{9,8},{10,11... | collective-permute-start | bytes 491528 | tf_op jit(solution)/shard_map/ppermute | solution.py:194
  2.7 0.0 copy-done
  2.7 0.9 %shard_map.28 = f32[640,128]{1,0:T(8,128)} custom-call(f32[640,128]{1,0:T(8,128)S(1)} %bitcast.11), custom_call_target="tpu_custom_call" | custom-call | bytes 1048576 | tf_op jit(solution)/shard_map/pallas_call | solution.py:202
  3.7 10.2 %all-to-all-start = ((f32[128,1,640]{2,1,0:T(1,128)}), f32[128,1,640]{2,1,0:T(1,128)S(1)}, u32[]{:S(2)}, u32[]{:S(2)}) async-start(f32[128,1,640]{2,1,0:T(1,128)} %bitcast.3), calls=%async_computation | async-start | bytes 655360 | tf_op jit(solution)/shard_map/all_to_all | solution.py:205
  13.9 0.0 collective-permute-done.other_ref
  14.0 2.9 %collective-permute-start.1 = (f32[320,128]{1,0:T(8,128)S(1)}, f32[320,128]{1,0:T(8,128)S(1)}, u32[]{:S(2)}, u32[]{:S(2)}) collective-permute-start(f32[320,128]{1,0:T(8,128)S(1)} %get-tuple-element.19), channel_id=1, source_target_pairs={{0,8},{2,10},{4,12},{6,14},{8,0},{10,2},{12,4},{14,6},{1,9},{3,11}... | collective-permute-start | bytes 491528 | tf_op jit(solution)/shard_map/ppermute | solution.py:194
  16.9 6.6 %collective-permute-done.1.refs_1_ = f32[320,128]{1,0:T(8,128)S(1)} collective-permute-done((f32[320,128]{1,0:T(8,128)S(1)}, f32[320,128]{1,0:T(8,128)S(1)}, u32[]{:S(2)}, u32[]{:S(2)}) %collective-permute-start.1) | collective-permute-done | bytes 163872 | tf_op jit(solution)/shard_map/ppermute | solution.py:194
  23.6 2.1 %collective-permute-start.2 = (f32[160,128]{1,0:T(8,128)S(1)}, f32[160,128]{1,0:T(8,128)S(1)}, u32[]{:S(2)}, u32[]{:S(2)}) collective-permute-start(f32[160,128]{1,0:T(8,128)S(1)} %get-tuple-element.21), channel_id=1, source_target_pairs={{0,2},{2,0},{4,6},{6,4},{8,10},{10,8},{12,14},{14,12},{1,3},{3,1},... | collective-permute-start | bytes 245768 | tf_op jit(solution)/shard_map/ppermute | solution.py:194
  25.7 3.2 %collective-permute-start.3 = (f32[160,128]{1,0:T(8,128)S(1)}, f32[160,128]{1,0:T(8,128)S(1)}, u32[]{:S(2)}, u32[]{:S(2)}) collective-permute-start(f32[160,128]{1,0:T(8,128)S(1)} %get-tuple-element.22), channel_id=1, source_target_pairs={{0,4},{2,6},{4,0},{6,2},{8,12},{10,14},{12,8},{14,10},{1,5},{3,7},... | collective-permute-start | bytes 245768 | tf_op jit(solution)/shard_map/ppermute | solution.py:194
  28.9 0.0 collective-permute-start.4
  28.9 0.4 shard_map.29.swapped_ref
  29.2 0.0 all-to-all-done
  29.2 0.0 collective-permute-done.2.w1
  29.3 2.8 %collective-permute-done.3.w2 = f32[160,128]{1,0:T(8,128)S(1)} collective-permute-done((f32[160,128]{1,0:T(8,128)S(1)}, f32[160,128]{1,0:T(8,128)S(1)}, u32[]{:S(2)}, u32[]{:S(2)}) %collective-permute-start.3) | collective-permute-done | bytes 81952 | tf_op jit(solution)/shard_map/ppermute | solution.py:194
  32.1 2.1 %collective-permute-done.4.w3 = f32[160,128]{1,0:T(8,128)S(1)} collective-permute-done((f32[160,128]{1,0:T(8,128)S(1)}, f32[160,128]{1,0:T(8,128)S(1)}, u32[]{:S(2)}, u32[]{:S(2)}) %collective-permute-start.4) | collective-permute-done | bytes 81952 | tf_op jit(solution)/shard_map/ppermute | solution.py:194
  34.2 1.5 %shard_map.33 = (f32[1024,128]{1,0:T(8,128)S(1)}, f32[256,384]{1,0:T(8,128)S(1)}, f32[3,512,128]{2,1,0:T(8,128)S(1)}) custom-call(f32[640,128]{1,0:T(8,128)S(1)} %bitcast.14, f32[640,128]{1,0:T(8,128)S(1)} %shard_map.29.swapped_ref, f32[160,128]{1,0:T(8,128)S(1)} %get-tuple-element.20.w0, f32[160,128]{1,0:T(8,128)S(1)} %collective-permute-done.2.w1, ...), custom_call_target="tpu_custom_call" | custom-call | flops 603979776 | bytes 1048576 | tf_op jit(solution)/shard_map/pallas_call | solution.py:213
  35.7 1.8 %collective-permute-start.5 = (f32[1024,128]{1,0:T(8,128)S(1)}, f32[1024,128]{1,0:T(8,128)S(1)}, u32[]{:S(2)}, u32[]{:S(2)}) collective-permute-start(f32[1024,128]{1,0:T(8,128)S(1)} %get-tuple-element.26), channel_id=1, source_target_pairs={{0,1},{1,0},{2,3},{3,2},{4,5},{5,4},{6,7},{7,6},{8,9},{9,8},{10,11... | collective-permute-start | bytes 1572872 | tf_op jit(solution)/shard_map/ppermute | solution.py:194
  37.4 1.1 %shard_map.34 = f32[1024,128]{1,0:T(8,128)S(1)} custom-call(f32[256,384]{1,0:T(8,128)S(1)} %get-tuple-element.24.p_ref, f32[3,512,128]{2,1,0:T(8,128)S(1)} %get-tuple-element.25.q_ref), custom_call_target="tpu_custom_call" | custom-call | flops 603979776 | bytes 1048576 | tf_op jit(solution)/shard_map/pallas_call | solution.py:224
  38.6 0.4 collective-permute-done.5
  39.0 0.1 add.3
  39.0 17.2 %all_to_all.10 = f32[64,16,128]{2,1,0:T(8,128)S(1)} all-to-all(f32[64,16,128]{2,1,0:T(8,128)S(1)} %bitcast.15), channel_id=1, replica_groups=mesh['row'=8,'yz'=8,'core'=2] {'row','yz'}, dimensions={0} | all-to-all | bytes 1048576 | tf_op jit(solution)/shard_map/all_to_all | solution.py:226
  56.2 0.7 %shard_map.35 = f32[4,512]{1,0:T(4,128)} custom-call(f32[1024,128]{1,0:T(8,128)S(1)} %bitcast.10), custom_call_target="tpu_custom_call" | custom-call | bytes 1048576 | tf_op jit(solution)/shard_map/pallas_call | solution.py:227
  (2 shorter events, 0.1 us)
Async XLA Ops:
  0.0 2.7 %copy-start = (f32[4,20480]{1,0:T(4,128)S(1)}, f32[4,20480]{1,0:T(4,128)}, u32[]{:S(2)}) copy-start(f32[4,20480]{1,0:T(4,128)} %param.2) | copy-start | bytes 983044
  0.0 1.0 %copy-start.1 = (f32[2560,32]{0,1:T(8,128)S(1)}, f32[2560,32]{0,1:T(8,128)}, u32[]{:S(2)}) copy-start(f32[2560,32]{0,1:T(8,128)} %param.3) | copy-start | bytes 983044
  1.3 12.6 %collective-permute-start = (f32[320,128]{1,0:T(8,128)S(1)}, f32[320,128]{1,0:T(8,128)S(1)}, u32[]{:S(2)}, u32[]{:S(2)}) collective-permute-start(f32[320,128]{1,0:T(8,128)S(1)} %get-tuple-element.17), channel_id=1, source_target_pairs={{0,1},{1,0},{2,3},{3,2},{4,5},{5,4},{6,7},{7,6},{8,9},{9,8},{10,11... | collective-permute-start | bytes 491528 | tf_op jit(solution)/shard_map/ppermute | solution.py:194
  3.7 25.6 %all-to-all-start = ((f32[128,1,640]{2,1,0:T(1,128)}), f32[128,1,640]{2,1,0:T(1,128)S(1)}, u32[]{:S(2)}, u32[]{:S(2)}) async-start(f32[128,1,640]{2,1,0:T(1,128)} %bitcast.3), calls=%async_computation | async-start | bytes 655360 | tf_op jit(solution)/shard_map/all_to_all | solution.py:205
  14.0 9.6 %collective-permute-start.1 = (f32[320,128]{1,0:T(8,128)S(1)}, f32[320,128]{1,0:T(8,128)S(1)}, u32[]{:S(2)}, u32[]{:S(2)}) collective-permute-start(f32[320,128]{1,0:T(8,128)S(1)} %get-tuple-element.19), channel_id=1, source_target_pairs={{0,8},{2,10},{4,12},{6,14},{8,0},{10,2},{12,4},{14,6},{1,9},{3,11}... | collective-permute-start | bytes 491528 | tf_op jit(solution)/shard_map/ppermute | solution.py:194
  23.6 5.7 %collective-permute-start.2 = (f32[160,128]{1,0:T(8,128)S(1)}, f32[160,128]{1,0:T(8,128)S(1)}, u32[]{:S(2)}, u32[]{:S(2)}) collective-permute-start(f32[160,128]{1,0:T(8,128)S(1)} %get-tuple-element.21), channel_id=1, source_target_pairs={{0,2},{2,0},{4,6},{6,4},{8,10},{10,8},{12,14},{14,12},{1,3},{3,1},... | collective-permute-start | bytes 245768 | tf_op jit(solution)/shard_map/ppermute | solution.py:194
  25.7 6.4 %collective-permute-start.3 = (f32[160,128]{1,0:T(8,128)S(1)}, f32[160,128]{1,0:T(8,128)S(1)}, u32[]{:S(2)}, u32[]{:S(2)}) collective-permute-start(f32[160,128]{1,0:T(8,128)S(1)} %get-tuple-element.22), channel_id=1, source_target_pairs={{0,4},{2,6},{4,0},{6,2},{8,12},{10,14},{12,8},{14,10},{1,5},{3,7},... | collective-permute-start | bytes 245768 | tf_op jit(solution)/shard_map/ppermute | solution.py:194
  28.9 5.3 %collective-permute-start.4 = (f32[160,128]{1,0:T(8,128)S(1)}, f32[160,128]{1,0:T(8,128)S(1)}, u32[]{:S(2)}, u32[]{:S(2)}) collective-permute-start(f32[160,128]{1,0:T(8,128)S(1)} %get-tuple-element.23), channel_id=1, source_target_pairs={{0,6},{2,4},{4,2},{6,0},{8,14},{10,12},{12,10},{14,8},{1,7},{3,5},... | collective-permute-start | bytes 245768 | tf_op jit(solution)/shard_map/ppermute | solution.py:194
  35.7 3.3 %collective-permute-start.5 = (f32[1024,128]{1,0:T(8,128)S(1)}, f32[1024,128]{1,0:T(8,128)S(1)}, u32[]{:S(2)}, u32[]{:S(2)}) collective-permute-start(f32[1024,128]{1,0:T(8,128)S(1)} %get-tuple-element.26), channel_id=1, source_target_pairs={{0,1},{1,0},{2,3},{3,2},{4,5},{5,4},{6,7},{7,6},{8,9},{9,8},{10,11... | collective-permute-start | bytes 1572872 | tf_op jit(solution)/shard_map/ppermute | solution.py:194

commit v3 on v2

--- a/solution.py
+++ b/solution.py
@@ -22,13 +22,17 @@
 F32 = jnp.float32
 
 
-def call(body, out_shapes, scratch=(), flops=0, moved=1 << 20):
+def call(body, out_shapes, scratch=(), flops=0, moved=1 << 20, **specs):
     several = isinstance(out_shapes, list)
-    outs = [jax.ShapeDtypeStruct(s, F32) for s in (out_shapes if several else [out_shapes])]
+    outs = [
+        s if isinstance(s, jax.ShapeDtypeStruct) else jax.ShapeDtypeStruct(s, F32)
+        for s in (out_shapes if several else [out_shapes])
+    ]
     return pl.pallas_call(
         body,
         out_shape=outs if several else outs[0],
         scratch_shapes=list(scratch),
+        **specs,
         cost_estimate=pl.CostEstimate(flops=flops, bytes_accessed=moved, transcendentals=0),
         compiler_params=pltpu.CompilerParams(vmem_limit_bytes=16 << 20),
     )
@@ -93,7 +97,12 @@
         out_ref[pl.ds(5 * j + 4, groups, stride=20), :] = rest
 
 
-def pack_cycle(w_ref, own_ref, other_ref, all_ref):
+def pack_cycle(w_hbm, m_hbm, own_ref, other_ref, m_ref, w_ref, all_ref, sems):
+    w_copy = pltpu.make_async_copy(w_hbm, w_ref, sems.at[0])
+    m_copy = pltpu.make_async_copy(m_hbm, m_ref, sems.at[1])
+    w_copy.start()
+    m_copy.start()
+    w_copy.wait()
     lane = lane_index(8)
     for e in range(2 * N_YZ):
         rest = None
@@ -108,6 +117,7 @@
     for yz in range(N_YZ):
         own_ref[chunk(yz), :] = all_ref[chunk(2 * yz + core), :]
         other_ref[chunk(yz), :] = all_ref[chunk(2 * yz + 1 - core), :]
+    m_copy.wait()
 
 
 def turn_far(own_ref, other_ref, *out_refs):
@@ -127,58 +137,68 @@
                 ref[chunk(2 * n + s), :] = piece[chunk(2 * (z ^ j) + s), :]
 
 
-def product(x, y):
-    return lax.dot_general(
-        x, y, (((1,), (1,)), ((), ())), precision=lax.Precision.HIGHEST, preferred_element_type=F32
-    )
+def split(x):
+    high = x.astype(jnp.bfloat16)
+    return high, (x - high.astype(F32)).astype(jnp.bfloat16)
+
+
+def left_side(parts):
+    high, low = split(jnp.concatenate(parts, axis=1))
+    return jnp.concatenate([high, high, low], axis=1)
+
+
+def right_side(parts):
+    high, low = split(jnp.concatenate(parts, axis=1))
+    return jnp.concatenate([high, low, high], axis=1)
 
 
 def half_update(p_ref, q_ref, out_ref):
-    term = product(p_ref[...], jnp.concatenate([q_ref[n] for n in range(3)], axis=1))
+    term = lax.dot_general(
+        p_ref[...], q_ref[...], (((1,), (1,)), ((), ())), preferred_element_type=F32
+    )
     for i in range(PER):
         for m in range(V // LANES):
             piece = term[CHIPS * i : CHIPS * i + CHIPS, LANES * m : LANES * m + LANES]
             out_ref[pl.ds(4 * m + i, CHIPS, stride=ROWS_OUT), :] = piece
 
 
-def first_half(got_ref, swapped_ref, w0, w1, w2, w3, out_ref, p_own, q_ref, x_ref, w_ref, p_ref):
+def arrange_slab(got_ref, swapped_ref, by_core_ref, by_row_ref, x_ref):
+    core = lax.axis_index("core")
+    x_ref[...] = 2.0 * got_ref[...] - swapped_ref[...]
+    for h, parity in enumerate((1 - core, core)):
+        packed = x_ref[pl.ds(5 * parity + 4, CHIPS, stride=10), :]
+        for i in range(PER):
+            parts = x_ref[pl.ds(5 * parity + i, CHIPS, stride=10), :], rolled(packed, -REST * i)
+            for n, part in enumerate(parts):
+                by_core_ref[n, h, CHIPS * i : CHIPS * i + CHIPS, :] = part
+                by_row_ref[n, pl.ds(4 * parity + i, CHIPS, stride=8), :] = part
+
+
+def first_half(a_core, a_row, w0, w1, w2, w3, out_ref, p_own, q_ref, w_ref, w_core, w_row, p_ref):
     me, core = lax.axis_index("yz"), lax.axis_index("core")
     for j, ref in enumerate((w0, w1, w2, w3)):
         for n, k in enumerate(FAR):
             for s in range(2):
                 w_ref[chunk(2 * (me ^ k ^ j) + (core ^ s)), :] = ref[chunk(2 * n + s), :]
-    x_ref[...] = 2.0 * got_ref[...] - swapped_ref[...]
-    lane = lane_index(CHIPS)
     n_row = DEVICES // (2 * N_YZ)
-    for parity, p_out in ((1 - core, p_ref), (core, p_own)):
-        packed = x_ref[pl.ds(5 * parity + 4, CHIPS, stride=10), :]
-        for i in range(PER):
-            a_main = x_ref[pl.ds(5 * parity + i, CHIPS, stride=10), :]
-            a_rest = rolled(packed, -REST * i)
-            w_main = jnp.concatenate(
-                [w_ref[pl.ds(CHUNK * parity + 4 * r + i, N_YZ, stride=2 * CHUNK), :] for r in range(n_row)], axis=0
-            )
-            w_rest = jnp.concatenate(
-                [
-                    rolled(
-                        w_ref[pl.ds(CHUNK * parity + 32 + 4 * (r % 2) + i, N_YZ, stride=2 * CHUNK), :],
-                        REST * (1 - r // 2),
-                    )
-                    for r in range(n_row)
-                ],
-                axis=0,
-            )
-            rows = slice(CHIPS * i, CHIPS * i + CHIPS)
-            spread = pl.ds(4 * parity + i, CHIPS, stride=8)
-            p_out[rows, :LANES] = a_main
-            p_out[rows, LANES : 2 * LANES] = w_main
-            q_ref[0, spread, :] = w_main
-            q_ref[1, spread, :] = a_main
-            p_out[rows, 2 * LANES :] = jnp.where(lane < REST, a_rest, jnp.where(lane < 2 * REST, w_rest, 0.0))
-            w_first, a_second = rolled(w_rest, -REST), rolled(a_rest, REST)
-            q_ref[2, spread, :] = jnp.where(
-                lane < REST, w_first, jnp.where(lane < 2 * REST, a_second, 0.0)
-            )
+    for h, parity in enumerate((1 - core, core)):
+        for i in range(PER):
+            for r in range(n_row):
+                first = CHUNK * parity + 4 * r + i, CHUNK * parity + 32 + 4 * (r % 2) + i
+                for n, at in enumerate(first):
+                    part = w_ref[pl.ds(at, N_YZ, stride=2 * CHUNK), :]
+                    part = rolled(part, -REST * (r // 2)) if n else part
+                    begin = CHIPS * i + N_YZ * r
+                    w_core[n, h, begin : begin + N_YZ, :] = part
+                    w_row[n, pl.ds(8 * N_YZ * r + 4 * parity + i, N_YZ, stride=8), :] = part
+
+    def both(x, y):
+        lane = lane_index(x.shape[0])
+        return jnp.where(lane < REST, x, jnp.where(lane < 2 * REST, rolled(y, REST), 0.0))
+
+    q_ref[...] = right_side([w_row[0], a_row[0], both(w_row[1], a_row[1])])
+    for h, ref in enumerate((p_ref, p_own)):
+        ref[...] = left_side([a_core[0, h], w_core[0, h], both(a_core[1, h], w_core[1, h])])
     half_update(p_ref, q_ref, out_ref)
 
 
@@ -197,7 +217,18 @@
 def on_device(multiplier, cycle_tiles):
     slab = multiplier.reshape(PER, DEPTH, LANES).transpose(1, 0, 2).reshape(PER * DEPTH, LANES)
     half, quarter = (N_YZ * CHUNK, LANES), (4 * CHUNK, LANES)
-    own, other = call(pack_cycle, [half] * 2, scratch=[VMEM((2 * N_YZ * CHUNK, LANES), F32)])(cycle_tiles.T)
+    columns = cycle_tiles.T
+    own, other, slab = call(
+        pack_cycle,
+        [half, half, slab.shape],
+        scratch=[
+            VMEM(columns.shape, F32),
+            VMEM((2 * N_YZ * CHUNK, LANES), F32),
+            pltpu.SemaphoreType.DMA((2,)),
+        ],
+        in_specs=[pl.BlockSpec(memory_space=pltpu.HBM)] * 2,
+        out_specs=[pl.BlockSpec(memory_space=VMEM)] * 3,
+    )(*(pltpu.with_memory_space_constraint(x, pltpu.HBM) for x in (columns, slab)))
     other = swap(other, "core", 1)
     packed = call(pack_multiplier, (5 * DEVICES, LANES))(slab)
     far = call(turn_far, [half] * 2)(own, other)
@@ -208,18 +239,24 @@
     near = call(turn_near, [quarter] * 4)(*far)
     near = [near[0], *(swap(x, "yz", j) for j, x in enumerate(near) if j)]
     swapped = call(pack_swapped, (5 * DEVICES, LANES))(slab)
-    width = 3 * LANES
-    rows, flops = CHIPS * ROWS_OUT, V * V * width * 6
+    width = 9 * LANES
+    rows, flops = CHIPS * ROWS_OUT, V * V * width
+    by_core, by_row = (2, 2, V // 2, LANES), (2, V, LANES)
+    a_core, a_row = call(arrange_slab, [by_core, by_row], scratch=[VMEM((5 * DEVICES, LANES), F32)])(
+        got.reshape(5 * DEVICES, LANES), swapped
+    )
+    sides = [jax.ShapeDtypeStruct((n, width), jnp.bfloat16) for n in (V // 2, V)]
     theirs, p_own, q = call(
         first_half,
-        [(rows, LANES), (V // 2, width), (3, V, LANES)],
+        [(rows, LANES), *sides],
         scratch=[
-            VMEM((5 * DEVICES, LANES), F32),
             VMEM((2 * N_YZ * CHUNK, LANES), F32),
-            VMEM((V // 2, width), F32),
+            VMEM(by_core, F32),
+            VMEM(by_row, F32),
+            VMEM((V // 2, width), jnp.bfloat16),
         ],
         flops=flops,
-    )(got.reshape(5 * DEVICES, LANES), swapped, *near)
+    )(a_core, a_row, *near)
     theirs = swap(theirs, "core", 1)
     mine = call(half_update, (rows, LANES), flops=flops)(p_own, q)
     share = mine + theirs

time: 57.7 us -> 57.3 us (level)
  local copies, waits for them, and re-layouts: 1.02 us -> 0 us
    unnamed x4 -> x0, local copies, waits for them, and re-layouts: 1.02 us -> none
    pallas_call x2 -> x3, Pallas kernels: 1.72 us -> 2.45 us  [the longest x1 1.27 us: on_device(): call(pack_cycle, [half, half, slab.shape], scratch=[VMEM(columns.shape, F...]
where the time goes in v3:
time: 57.3 us; the launch traced here: 56.5 us
  starting transfers between devices  21.7 us (38%)
  blocking collectives  17.2 us (30%)
  waiting for transfers between devices  12.3 us (21%)
  Pallas kernels  5.11 us (9%)
    all_to_all x1, blocking collectives, on_device(): lax.all_to_all(share.reshape(CHIPS, ROWS_OUT, LANES), ('row', 'yz'), 0, 0...  17.2 us
    ppermute x6, waiting for transfers between devices, swap(): lax.ppermute(x, axis, [(n, n ^ k) for n in range(lax.axis_size(axis))])  12.3 us
    ppermute x6, starting transfers between devices, swap(): lax.ppermute(x, axis, [(n, n ^ k) for n in range(lax.axis_size(axis))])  11.5 us
    all_to_all x1, starting transfers between devices, on_device(): lax.all_to_all(packed.reshape(DEVICES, 1, 5 * LANES), ('row', 'yz', 'core...  10.2 us
    pallas_call x1, Pallas kernels, on_device(): call(pack_cycle, [half, half, slab.shape], scratch=[VMEM(columns.shape, F...  1.27 us
  transfers between devices with their start and end apart: 7, of which 4 were waited for; matrix products, arithmetic and copies ran while one was open for 0% of the time, Pallas kernels for 4%

profile of v3, /device:TPU:1, one launch (start us, length us, event | category | flops | bytes accessed | tf_op | source)
XLA Modules:
  0.0 56.5 jit_solution(1400279876473104186)
XLA Ops:
  0.0 1.3 %shard_map.28 = (f32[320,128]{1,0:T(8,128)S(1)}, f32[320,128]{1,0:T(8,128)S(1)}, f32[640,128]{1,0:T(8,128)S(1)}) custom-call(f32[32,2560]{1,0:T(8,128)} %bitcast.13, f32[640,128]{1,0:T(8,128)} %bitcast.14), custom_call_target="tpu_custom_call" | custom-call | bytes 1048576 | tf_op jit(solution)/shard_map/pallas_call | solution.py:221
  1.3 1.4 %collective-permute-start = (f32[320,128]{1,0:T(8,128)S(1)}, f32[320,128]{1,0:T(8,128)S(1)}, u32[]{:S(2)}, u32[]{:S(2)}) collective-permute-start(f32[320,128]{1,0:T(8,128)S(1)} %get-tuple-element.23), channel_id=1, source_target_pairs={{0,1},{1,0},{2,3},{3,2},{4,5},{5,4},{6,7},{7,6},{8,9},{9,8},{10,11... | collective-permute-start | bytes 491528 | tf_op jit(solution)/shard_map/ppermute | solution.py:214
  2.7 0.9 %shard_map.29 = f32[640,128]{1,0:T(8,128)} custom-call(f32[640,128]{1,0:T(8,128)S(1)} %get-tuple-element.19.m_ref), custom_call_target="tpu_custom_call" | custom-call | bytes 1048576 | tf_op jit(solution)/shard_map/pallas_call | solution.py:233
  3.7 10.2 %all-to-all-start = ((f32[128,1,640]{2,1,0:T(1,128)}), f32[128,1,640]{2,1,0:T(1,128)S(1)}, u32[]{:S(2)}, u32[]{:S(2)}) async-start(f32[128,1,640]{2,1,0:T(1,128)} %bitcast.4), calls=%async_computation | async-start | bytes 655360 | tf_op jit(solution)/shard_map/all_to_all | solution.py:236
  13.9 0.0 collective-permute-done.other_ref
  13.9 2.9 %collective-permute-start.1 = (f32[320,128]{1,0:T(8,128)S(1)}, f32[320,128]{1,0:T(8,128)S(1)}, u32[]{:S(2)}, u32[]{:S(2)}) collective-permute-start(f32[320,128]{1,0:T(8,128)S(1)} %get-tuple-element.25), channel_id=1, source_target_pairs={{0,8},{2,10},{4,12},{6,14},{8,0},{10,2},{12,4},{14,6},{1,9},{3,11}... | collective-permute-start | bytes 491528 | tf_op jit(solution)/shard_map/ppermute | solution.py:214
  16.9 6.6 %collective-permute-done.1.refs_1_ = f32[320,128]{1,0:T(8,128)S(1)} collective-permute-done((f32[320,128]{1,0:T(8,128)S(1)}, f32[320,128]{1,0:T(8,128)S(1)}, u32[]{:S(2)}, u32[]{:S(2)}) %collective-permute-start.1) | collective-permute-done | bytes 163872 | tf_op jit(solution)/shard_map/ppermute | solution.py:214
  23.5 2.1 %collective-permute-start.2 = (f32[160,128]{1,0:T(8,128)S(1)}, f32[160,128]{1,0:T(8,128)S(1)}, u32[]{:S(2)}, u32[]{:S(2)}) collective-permute-start(f32[160,128]{1,0:T(8,128)S(1)} %get-tuple-element.27), channel_id=1, source_target_pairs={{0,2},{2,0},{4,6},{6,4},{8,10},{10,8},{12,14},{14,12},{1,3},{3,1},... | collective-permute-start | bytes 245768 | tf_op jit(solution)/shard_map/ppermute | solution.py:214
  25.7 3.2 %collective-permute-start.3 = (f32[160,128]{1,0:T(8,128)S(1)}, f32[160,128]{1,0:T(8,128)S(1)}, u32[]{:S(2)}, u32[]{:S(2)}) collective-permute-start(f32[160,128]{1,0:T(8,128)S(1)} %get-tuple-element.28), channel_id=1, source_target_pairs={{0,4},{2,6},{4,0},{6,2},{8,12},{10,14},{12,8},{14,10},{1,5},{3,7},... | collective-permute-start | bytes 245768 | tf_op jit(solution)/shard_map/ppermute | solution.py:214
  28.8 0.0 collective-permute-start.4
  28.8 0.4 shard_map.30.swapped_ref
  29.2 0.0 all-to-all-done
  29.2 0.2 shard_map.31
  29.4 0.0 collective-permute-done.2.w1
  29.4 2.6 %collective-permute-done.3.w2 = f32[160,128]{1,0:T(8,128)S(1)} collective-permute-done((f32[160,128]{1,0:T(8,128)S(1)}, f32[160,128]{1,0:T(8,128)S(1)}, u32[]{:S(2)}, u32[]{:S(2)}) %collective-permute-start.3) | collective-permute-done | bytes 81952 | tf_op jit(solution)/shard_map/ppermute | solution.py:214
  32.0 2.1 %collective-permute-done.4.w3 = f32[160,128]{1,0:T(8,128)S(1)} collective-permute-done((f32[160,128]{1,0:T(8,128)S(1)}, f32[160,128]{1,0:T(8,128)S(1)}, u32[]{:S(2)}, u32[]{:S(2)}) %collective-permute-start.4) | collective-permute-done | bytes 81952 | tf_op jit(solution)/shard_map/ppermute | solution.py:214
  34.2 1.0 %shard_map.34 = (f32[1024,128]{1,0:T(8,128)S(1)}, bf16[256,1152]{1,0:T(8,128)(2,1)S(1)}, bf16[512,1152]{1,0:T(8,128)(2,1)S(1)}) custom-call(f32[2,2,256,128]{3,2,1,0:T(8,128)S(1)} %get-tuple-element.20.a_core, f32[2,512,128]{2,1,0:T(8,128)S(1)} %get-tuple-element.21.a_row, f32[160,128]{1,0:T(8,128)S(1)} %get-tuple-element.26.w0, ...), custom_call_target="tpu_custom_call" | custom-call | flops 301989888 | bytes 1048576 | tf_op jit(solution)/shard_map/pallas_call | solution.py:249
  35.2 1.8 %collective-permute-start.5 = (f32[1024,128]{1,0:T(8,128)S(1)}, f32[1024,128]{1,0:T(8,128)S(1)}, u32[]{:S(2)}, u32[]{:S(2)}) collective-permute-start(f32[1024,128]{1,0:T(8,128)S(1)} %get-tuple-element.32), channel_id=1, source_target_pairs={{0,1},{1,0},{2,3},{3,2},{4,5},{5,4},{6,7},{7,6},{8,9},{9,8},{10,11... | collective-permute-start | bytes 1572872 | tf_op jit(solution)/shard_map/ppermute | solution.py:214
  37.0 0.6 %shard_map.35 = f32[1024,128]{1,0:T(8,128)S(1)} custom-call(bf16[256,1152]{1,0:T(8,128)(2,1)S(1)} %get-tuple-element.30.p_ref, bf16[512,1152]{1,0:T(8,128)(2,1)S(1)} %get-tuple-element.31.q_ref), custom_call_target="tpu_custom_call" | custom-call | flops 301989888 | bytes 1048576 | tf_op jit(solution)/shard_map/pallas_call | solution.py:261
  37.6 0.9 %collective-permute-done.5 = f32[1024,128]{1,0:T(8,128)S(1)} collective-permute-done((f32[1024,128]{1,0:T(8,128)S(1)}, f32[1024,128]{1,0:T(8,128)S(1)}, u32[]{:S(2)}, u32[]{:S(2)}) %collective-permute-start.5) | collective-permute-done | bytes 524320 | tf_op jit(solution)/shard_map/ppermute | solution.py:214
  38.5 0.1 add.3
  38.6 17.2 %all_to_all.10 = f32[64,16,128]{2,1,0:T(8,128)S(1)} all-to-all(f32[64,16,128]{2,1,0:T(8,128)S(1)} %bitcast.12), channel_id=1, replica_groups=mesh['row'=8,'yz'=8,'core'=2] {'row','yz'}, dimensions={0} | all-to-all | bytes 1048576 | tf_op jit(solution)/shard_map/all_to_all | solution.py:263
  55.8 0.7 %shard_map.36 = f32[4,512]{1,0:T(4,128)} custom-call(f32[1024,128]{1,0:T(8,128)S(1)} %bitcast.10), custom_call_target="tpu_custom_call" | custom-call | bytes 1048576 | tf_op jit(solution)/shard_map/pallas_call | solution.py:264
  (2 shorter events, 0.1 us)
Async XLA Ops:
  1.3 12.6 %collective-permute-start = (f32[320,128]{1,0:T(8,128)S(1)}, f32[320,128]{1,0:T(8,128)S(1)}, u32[]{:S(2)}, u32[]{:S(2)}) collective-permute-start(f32[320,128]{1,0:T(8,128)S(1)} %get-tuple-element.23), channel_id=1, source_target_pairs={{0,1},{1,0},{2,3},{3,2},{4,5},{5,4},{6,7},{7,6},{8,9},{9,8},{10,11... | collective-permute-start | bytes 491528 | tf_op jit(solution)/shard_map/ppermute | solution.py:214
  3.7 25.6 %all-to-all-start = ((f32[128,1,640]{2,1,0:T(1,128)}), f32[128,1,640]{2,1,0:T(1,128)S(1)}, u32[]{:S(2)}, u32[]{:S(2)}) async-start(f32[128,1,640]{2,1,0:T(1,128)} %bitcast.4), calls=%async_computation | async-start | bytes 655360 | tf_op jit(solution)/shard_map/all_to_all | solution.py:236
  13.9 9.6 %collective-permute-start.1 = (f32[320,128]{1,0:T(8,128)S(1)}, f32[320,128]{1,0:T(8,128)S(1)}, u32[]{:S(2)}, u32[]{:S(2)}) collective-permute-start(f32[320,128]{1,0:T(8,128)S(1)} %get-tuple-element.25), channel_id=1, source_target_pairs={{0,8},{2,10},{4,12},{6,14},{8,0},{10,2},{12,4},{14,6},{1,9},{3,11}... | collective-permute-start | bytes 491528 | tf_op jit(solution)/shard_map/ppermute | solution.py:214
  23.5 5.9 %collective-permute-start.2 = (f32[160,128]{1,0:T(8,128)S(1)}, f32[160,128]{1,0:T(8,128)S(1)}, u32[]{:S(2)}, u32[]{:S(2)}) collective-permute-start(f32[160,128]{1,0:T(8,128)S(1)} %get-tuple-element.27), channel_id=1, source_target_pairs={{0,2},{2,0},{4,6},{6,4},{8,10},{10,8},{12,14},{14,12},{1,3},{3,1},... | collective-permute-start | bytes 245768 | tf_op jit(solution)/shard_map/ppermute | solution.py:214
  25.7 6.4 %collective-permute-start.3 = (f32[160,128]{1,0:T(8,128)S(1)}, f32[160,128]{1,0:T(8,128)S(1)}, u32[]{:S(2)}, u32[]{:S(2)}) collective-permute-start(f32[160,128]{1,0:T(8,128)S(1)} %get-tuple-element.28), channel_id=1, source_target_pairs={{0,4},{2,6},{4,0},{6,2},{8,12},{10,14},{12,8},{14,10},{1,5},{3,7},... | collective-permute-start | bytes 245768 | tf_op jit(solution)/shard_map/ppermute | solution.py:214
  28.8 5.3 %collective-permute-start.4 = (f32[160,128]{1,0:T(8,128)S(1)}, f32[160,128]{1,0:T(8,128)S(1)}, u32[]{:S(2)}, u32[]{:S(2)}) collective-permute-start(f32[160,128]{1,0:T(8,128)S(1)} %get-tuple-element.29), channel_id=1, source_target_pairs={{0,6},{2,4},{4,2},{6,0},{8,14},{10,12},{12,10},{14,8},{1,7},{3,5},... | collective-permute-start | bytes 245768 | tf_op jit(solution)/shard_map/ppermute | solution.py:214
  35.2 3.3 %collective-permute-start.5 = (f32[1024,128]{1,0:T(8,128)S(1)}, f32[1024,128]{1,0:T(8,128)S(1)}, u32[]{:S(2)}, u32[]{:S(2)}) collective-permute-start(f32[1024,128]{1,0:T(8,128)S(1)} %get-tuple-element.32), channel_id=1, source_target_pairs={{0,1},{1,0},{2,3},{3,2},{4,5},{5,4},{6,7},{7,6},{8,9},{9,8},{10,11... | collective-permute-start | bytes 1572872 | tf_op jit(solution)/shard_map/ppermute | solution.py:214

commit v4 on v3

--- a/solution.py
+++ b/solution.py
@@ -103,16 +103,17 @@
     w_copy.start()
     m_copy.start()
     w_copy.wait()
+    rest = [None] * (2 * N_YZ)
     lane = lane_index(8)
-    for e in range(2 * N_YZ):
-        rest = None
-        for g in range(PER):
+    for g in range(PER):
+        for e in range(2 * N_YZ):
             piece = lambda n, g=g: w_ref[8 * g : 8 * g + 8, LANES * n : LANES * n + LANES]
             all_ref[CHUNK * e + 8 * g : CHUNK * e + 8 * g + 8, :] = window(piece, DEPTH * e, 8)
             first, off = divmod(DEPTH * e + LANES, LANES)
             tail = rolled(piece(first), REST * g - off)
-            rest = tail if rest is None else jnp.where(lane >= REST * g, tail, rest)
-        all_ref[CHUNK * e + 32 : CHUNK * e + 40, :] = rest
+            rest[e] = tail if g == 0 else jnp.where(lane >= REST * g, tail, rest[e])
+    for e in range(2 * N_YZ):
+        all_ref[CHUNK * e + 32 : CHUNK * e + 40, :] = rest[e]
     core = lax.axis_index("core")
     for yz in range(N_YZ):
         own_ref[chunk(yz), :] = all_ref[chunk(2 * yz + core), :]
@@ -142,14 +143,24 @@
     return high, (x - high.astype(F32)).astype(jnp.bfloat16)
 
 
-def left_side(parts):
-    high, low = split(jnp.concatenate(parts, axis=1))
-    return jnp.concatenate([high, high, low], axis=1)
-
-
-def right_side(parts):
-    high, low = split(jnp.concatenate(parts, axis=1))
-    return jnp.concatenate([high, low, high], axis=1)
+def rest_side(x, y, swapped):
+    lane = lane_index(x.shape[0])
+    both = jnp.where(lane < REST, x, rolled(y, REST))
+    high, low = split(jnp.where(lane < 2 * REST, both, 0.0))
+    wide = high.astype(F32), low.astype(F32)
+    first, second = (wide[0], wide[0]) if swapped else wide
+    third = low if swapped else high
+    return [(first + rolled(second, LANES // 2)).astype(jnp.bfloat16), third]
+
+
+def left_side(slab, cycle, slab_rest, cycle_rest):
+    (a, a_low), (w, w_low) = split(slab), split(cycle)
+    return jnp.concatenate([a, a_low, w, w_low, a, w, *rest_side(slab_rest, cycle_rest, False)], axis=1)
+
+
+def right_side(cycle, slab, cycle_rest, slab_rest):
+    (w, w_low), (a, a_low) = split(cycle), split(slab)
+    return jnp.concatenate([w, w, a, a, w_low, a_low, *rest_side(cycle_rest, slab_rest, True)], axis=1)
 
 
 def half_update(p_ref, q_ref, out_ref):
@@ -174,7 +185,7 @@
                 by_row_ref[n, pl.ds(4 * parity + i, CHIPS, stride=8), :] = part
 
 
-def first_half(a_core, a_row, w0, w1, w2, w3, out_ref, p_own, q_ref, w_ref, w_core, w_row, p_ref):
+def first_half(a_core, a_row, w0, w1, w2, w3, out_ref, w_core, q_ref, w_ref, w_row, p_ref):
     me, core = lax.axis_index("yz"), lax.axis_index("core")
     for j, ref in enumerate((w0, w1, w2, w3)):
         for n, k in enumerate(FAR):
@@ -192,13 +203,13 @@
                     w_core[n, h, begin : begin + N_YZ, :] = part
                     w_row[n, pl.ds(8 * N_YZ * r + 4 * parity + i, N_YZ, stride=8), :] = part
 
-    def both(x, y):
-        lane = lane_index(x.shape[0])
-        return jnp.where(lane < REST, x, jnp.where(lane < 2 * REST, rolled(y, REST), 0.0))
-
-    q_ref[...] = right_side([w_row[0], a_row[0], both(w_row[1], a_row[1])])
-    for h, ref in enumerate((p_ref, p_own)):
-        ref[...] = left_side([a_core[0, h], w_core[0, h], both(a_core[1, h], w_core[1, h])])
+    q_ref[...] = right_side(w_row[0], a_row[0], w_row[1], a_row[1])
+    p_ref[...] = left_side(a_core[0, 0], w_core[0, 0], a_core[1, 0], w_core[1, 0])
+    half_update(p_ref, q_ref, out_ref)
+
+
+def second_half(a_core, w_core, q_ref, out_ref, p_ref):
+    p_ref[...] = left_side(a_core[0, 1], w_core[0, 1], a_core[1, 1], w_core[1, 1])
     half_update(p_ref, q_ref, out_ref)
 
 
@@ -239,26 +250,21 @@
     near = call(turn_near, [quarter] * 4)(*far)
     near = [near[0], *(swap(x, "yz", j) for j, x in enumerate(near) if j)]
     swapped = call(pack_swapped, (5 * DEVICES, LANES))(slab)
-    width = 9 * LANES
+    width = 8 * LANES
     rows, flops = CHIPS * ROWS_OUT, V * V * width
     by_core, by_row = (2, 2, V // 2, LANES), (2, V, LANES)
     a_core, a_row = call(arrange_slab, [by_core, by_row], scratch=[VMEM((5 * DEVICES, LANES), F32)])(
         got.reshape(5 * DEVICES, LANES), swapped
     )
-    sides = [jax.ShapeDtypeStruct((n, width), jnp.bfloat16) for n in (V // 2, V)]
-    theirs, p_own, q = call(
+    left = VMEM((V // 2, width), jnp.bfloat16)
+    theirs, w_core, q = call(
         first_half,
-        [(rows, LANES), *sides],
-        scratch=[
-            VMEM((2 * N_YZ * CHUNK, LANES), F32),
-            VMEM(by_core, F32),
-            VMEM(by_row, F32),
-            VMEM((V // 2, width), jnp.bfloat16),
-        ],
+        [(rows, LANES), by_core, jax.ShapeDtypeStruct((V, width), jnp.bfloat16)],
+        scratch=[VMEM((2 * N_YZ * CHUNK, LANES), F32), VMEM(by_row, F32), left],
         flops=flops,
     )(a_core, a_row, *near)
     theirs = swap(theirs, "core", 1)
-    mine = call(half_update, (rows, LANES), flops=flops)(p_own, q)
+    mine = call(second_half, (rows, LANES), scratch=[left], flops=flops)(a_core, w_core, q)
     share = mine + theirs
     parts = lax.all_to_all(share.reshape(CHIPS, ROWS_OUT, LANES), ("row", "yz"), 0, 0, tiled=True)
     return call(finish, (PER, V))(parts.reshape(rows, LANES))

time: 57.3 us -> 57.1 us (level)
  no operation moved by 1% of the time
where the time goes in v4:
time: 57.1 us; the launch traced here: 56.3 us
  starting transfers between devices  21.7 us (38%)
  blocking collectives  17.2 us (30%)
  waiting for transfers between devices  12.4 us (22%)
  Pallas kernels  4.9 us (9%)
    all_to_all x1, blocking collectives, on_device(): lax.all_to_all(share.reshape(CHIPS, ROWS_OUT, LANES), ('row', 'yz'), 0, 0...  17.2 us
    ppermute x6, waiting for transfers between devices, swap(): lax.ppermute(x, axis, [(n, n ^ k) for n in range(lax.axis_size(axis))])  12.4 us
    ppermute x6, starting transfers between devices, swap(): lax.ppermute(x, axis, [(n, n ^ k) for n in range(lax.axis_size(axis))])  11.5 us
    all_to_all x1, starting transfers between devices, on_device(): lax.all_to_all(packed.reshape(DEVICES, 1, 5 * LANES), ('row', 'yz', 'core...  10.2 us
    pallas_call x1, Pallas kernels, on_device(): call(pack_cycle, [half, half, slab.shape], scratch=[VMEM(columns.shape, F...  1.26 us
  transfers between devices with their start and end apart: 7, of which 4 were waited for; matrix products, arithmetic and copies ran while one was open for 0% of the time, Pallas kernels for 4%

profile of v4, /device:TPU:1, one launch (start us, length us, event | category | flops | bytes accessed | tf_op | source)
XLA Modules:
  0.0 56.3 jit_solution(6600251138990989103)
XLA Ops:
  0.0 1.3 %shard_map.28 = (f32[320,128]{1,0:T(8,128)S(1)}, f32[320,128]{1,0:T(8,128)S(1)}, f32[640,128]{1,0:T(8,128)S(1)}) custom-call(f32[32,2560]{1,0:T(8,128)} %bitcast.13, f32[640,128]{1,0:T(8,128)} %bitcast.14), custom_call_target="tpu_custom_call" | custom-call | bytes 1048576 | tf_op jit(solution)/shard_map/pallas_call | solution.py:232
  1.3 1.4 %collective-permute-start = (f32[320,128]{1,0:T(8,128)S(1)}, f32[320,128]{1,0:T(8,128)S(1)}, u32[]{:S(2)}, u32[]{:S(2)}) collective-permute-start(f32[320,128]{1,0:T(8,128)S(1)} %get-tuple-element.23), channel_id=1, source_target_pairs={{0,1},{1,0},{2,3},{3,2},{4,5},{5,4},{6,7},{7,6},{8,9},{9,8},{10,11... | collective-permute-start | bytes 491528 | tf_op jit(solution)/shard_map/ppermute | solution.py:225
  2.7 0.9 %shard_map.29 = f32[640,128]{1,0:T(8,128)} custom-call(f32[640,128]{1,0:T(8,128)S(1)} %get-tuple-element.19.m_ref), custom_call_target="tpu_custom_call" | custom-call | bytes 1048576 | tf_op jit(solution)/shard_map/pallas_call | solution.py:244
  3.7 10.2 %all-to-all-start = ((f32[128,1,640]{2,1,0:T(1,128)}), f32[128,1,640]{2,1,0:T(1,128)S(1)}, u32[]{:S(2)}, u32[]{:S(2)}) async-start(f32[128,1,640]{2,1,0:T(1,128)} %bitcast.4), calls=%async_computation | async-start | bytes 655360 | tf_op jit(solution)/shard_map/all_to_all | solution.py:247
  13.9 0.0 collective-permute-done.other_ref
  13.9 2.9 %collective-permute-start.1 = (f32[320,128]{1,0:T(8,128)S(1)}, f32[320,128]{1,0:T(8,128)S(1)}, u32[]{:S(2)}, u32[]{:S(2)}) collective-permute-start(f32[320,128]{1,0:T(8,128)S(1)} %get-tuple-element.25), channel_id=1, source_target_pairs={{0,8},{2,10},{4,12},{6,14},{8,0},{10,2},{12,4},{14,6},{1,9},{3,11}... | collective-permute-start | bytes 491528 | tf_op jit(solution)/shard_map/ppermute | solution.py:225
  16.9 6.6 %collective-permute-done.1.refs_1_ = f32[320,128]{1,0:T(8,128)S(1)} collective-permute-done((f32[320,128]{1,0:T(8,128)S(1)}, f32[320,128]{1,0:T(8,128)S(1)}, u32[]{:S(2)}, u32[]{:S(2)}) %collective-permute-start.1) | collective-permute-done | bytes 163872 | tf_op jit(solution)/shard_map/ppermute | solution.py:225
  23.5 2.1 %collective-permute-start.2 = (f32[160,128]{1,0:T(8,128)S(1)}, f32[160,128]{1,0:T(8,128)S(1)}, u32[]{:S(2)}, u32[]{:S(2)}) collective-permute-start(f32[160,128]{1,0:T(8,128)S(1)} %get-tuple-element.27), channel_id=1, source_target_pairs={{0,2},{2,0},{4,6},{6,4},{8,10},{10,8},{12,14},{14,12},{1,3},{3,1},... | collective-permute-start | bytes 245768 | tf_op jit(solution)/shard_map/ppermute | solution.py:225
  25.7 3.2 %collective-permute-start.3 = (f32[160,128]{1,0:T(8,128)S(1)}, f32[160,128]{1,0:T(8,128)S(1)}, u32[]{:S(2)}, u32[]{:S(2)}) collective-permute-start(f32[160,128]{1,0:T(8,128)S(1)} %get-tuple-element.28), channel_id=1, source_target_pairs={{0,4},{2,6},{4,0},{6,2},{8,12},{10,14},{12,8},{14,10},{1,5},{3,7},... | collective-permute-start | bytes 245768 | tf_op jit(solution)/shard_map/ppermute | solution.py:225
  28.8 0.0 collective-permute-start.4
  28.8 0.4 shard_map.30.swapped_ref
  29.2 0.0 all-to-all-done
  29.2 0.2 shard_map.31
  29.4 0.0 collective-permute-done.2.w1
  29.4 2.6 %collective-permute-done.3.w2 = f32[160,128]{1,0:T(8,128)S(1)} collective-permute-done((f32[160,128]{1,0:T(8,128)S(1)}, f32[160,128]{1,0:T(8,128)S(1)}, u32[]{:S(2)}, u32[]{:S(2)}) %collective-permute-start.3) | collective-permute-done | bytes 81952 | tf_op jit(solution)/shard_map/ppermute | solution.py:225
  32.0 2.1 %collective-permute-done.4.w3 = f32[160,128]{1,0:T(8,128)S(1)} collective-permute-done((f32[160,128]{1,0:T(8,128)S(1)}, f32[160,128]{1,0:T(8,128)S(1)}, u32[]{:S(2)}, u32[]{:S(2)}) %collective-permute-start.4) | collective-permute-done | bytes 81952 | tf_op jit(solution)/shard_map/ppermute | solution.py:225
  34.2 0.9 %shard_map.34 = (f32[1024,128]{1,0:T(8,128)S(1)}, f32[2,2,256,128]{3,2,1,0:T(8,128)S(1)}, bf16[512,1024]{1,0:T(8,128)(2,1)S(1)}) custom-call(f32[2,2,256,128]{3,2,1,0:T(8,128)S(1)} %get-tuple-element.20.a_core, f32[2,512,128]{2,1,0:T(8,128)S(1)} %get-tuple-element.21.a_row, f32[160,128]{1,0:T(8,128)S(1)} %get-tuple-element.26.w0, ...), custom_call_target="tpu_custom_call" | custom-call | flops 268435456 | bytes 1048576 | tf_op jit(solution)/shard_map/pallas_call | solution.py:260
  35.1 1.8 %collective-permute-start.5 = (f32[1024,128]{1,0:T(8,128)S(1)}, f32[1024,128]{1,0:T(8,128)S(1)}, u32[]{:S(2)}, u32[]{:S(2)}) collective-permute-start(f32[1024,128]{1,0:T(8,128)S(1)} %get-tuple-element.32), channel_id=1, source_target_pairs={{0,1},{1,0},{2,3},{3,2},{4,5},{5,4},{6,7},{7,6},{8,9},{9,8},{10,11... | collective-permute-start | bytes 1572872 | tf_op jit(solution)/shard_map/ppermute | solution.py:225
  36.8 0.6 shard_map.35
  37.4 1.0 %collective-permute-done.5 = f32[1024,128]{1,0:T(8,128)S(1)} collective-permute-done((f32[1024,128]{1,0:T(8,128)S(1)}, f32[1024,128]{1,0:T(8,128)S(1)}, u32[]{:S(2)}, u32[]{:S(2)}) %collective-permute-start.5) | collective-permute-done | bytes 524320 | tf_op jit(solution)/shard_map/ppermute | solution.py:225
  38.4 0.1 add.3
  38.4 17.2 %all_to_all.10 = f32[64,16,128]{2,1,0:T(8,128)S(1)} all-to-all(f32[64,16,128]{2,1,0:T(8,128)S(1)} %bitcast.12), channel_id=1, replica_groups=mesh['row'=8,'yz'=8,'core'=2] {'row','yz'}, dimensions={0} | all-to-all | bytes 1048576 | tf_op jit(solution)/shard_map/all_to_all | solution.py:269
  55.6 0.7 %shard_map.36 = f32[4,512]{1,0:T(4,128)} custom-call(f32[1024,128]{1,0:T(8,128)S(1)} %bitcast.10), custom_call_target="tpu_custom_call" | custom-call | bytes 1048576 | tf_op jit(solution)/shard_map/pallas_call | solution.py:270
  (2 shorter events, 0.1 us)
Async XLA Ops:
  1.3 12.6 %collective-permute-start = (f32[320,128]{1,0:T(8,128)S(1)}, f32[320,128]{1,0:T(8,128)S(1)}, u32[]{:S(2)}, u32[]{:S(2)}) collective-permute-start(f32[320,128]{1,0:T(8,128)S(1)} %get-tuple-element.23), channel_id=1, source_target_pairs={{0,1},{1,0},{2,3},{3,2},{4,5},{5,4},{6,7},{7,6},{8,9},{9,8},{10,11... | collective-permute-start | bytes 491528 | tf_op jit(solution)/shard_map/ppermute | solution.py:225
  3.7 25.6 %all-to-all-start = ((f32[128,1,640]{2,1,0:T(1,128)}), f32[128,1,640]{2,1,0:T(1,128)S(1)}, u32[]{:S(2)}, u32[]{:S(2)}) async-start(f32[128,1,640]{2,1,0:T(1,128)} %bitcast.4), calls=%async_computation | async-start | bytes 655360 | tf_op jit(solution)/shard_map/all_to_all | solution.py:247
  13.9 9.6 %collective-permute-start.1 = (f32[320,128]{1,0:T(8,128)S(1)}, f32[320,128]{1,0:T(8,128)S(1)}, u32[]{:S(2)}, u32[]{:S(2)}) collective-permute-start(f32[320,128]{1,0:T(8,128)S(1)} %get-tuple-element.25), channel_id=1, source_target_pairs={{0,8},{2,10},{4,12},{6,14},{8,0},{10,2},{12,4},{14,6},{1,9},{3,11}... | collective-permute-start | bytes 491528 | tf_op jit(solution)/shard_map/ppermute | solution.py:225
  23.5 5.9 %collective-permute-start.2 = (f32[160,128]{1,0:T(8,128)S(1)}, f32[160,128]{1,0:T(8,128)S(1)}, u32[]{:S(2)}, u32[]{:S(2)}) collective-permute-start(f32[160,128]{1,0:T(8,128)S(1)} %get-tuple-element.27), channel_id=1, source_target_pairs={{0,2},{2,0},{4,6},{6,4},{8,10},{10,8},{12,14},{14,12},{1,3},{3,1},... | collective-permute-start | bytes 245768 | tf_op jit(solution)/shard_map/ppermute | solution.py:225
  25.7 6.4 %collective-permute-start.3 = (f32[160,128]{1,0:T(8,128)S(1)}, f32[160,128]{1,0:T(8,128)S(1)}, u32[]{:S(2)}, u32[]{:S(2)}) collective-permute-start(f32[160,128]{1,0:T(8,128)S(1)} %get-tuple-element.28), channel_id=1, source_target_pairs={{0,4},{2,6},{4,0},{6,2},{8,12},{10,14},{12,8},{14,10},{1,5},{3,7},... | collective-permute-start | bytes 245768 | tf_op jit(solution)/shard_map/ppermute | solution.py:225
  28.8 5.3 %collective-permute-start.4 = (f32[160,128]{1,0:T(8,128)S(1)}, f32[160,128]{1,0:T(8,128)S(1)}, u32[]{:S(2)}, u32[]{:S(2)}) collective-permute-start(f32[160,128]{1,0:T(8,128)S(1)} %get-tuple-element.29), channel_id=1, source_target_pairs={{0,6},{2,4},{4,2},{6,0},{8,14},{10,12},{12,10},{14,8},{1,7},{3,5},... | collective-permute-start | bytes 245768 | tf_op jit(solution)/shard_map/ppermute | solution.py:225
  35.1 3.3 %collective-permute-start.5 = (f32[1024,128]{1,0:T(8,128)S(1)}, f32[1024,128]{1,0:T(8,128)S(1)}, u32[]{:S(2)}, u32[]{:S(2)}) collective-permute-start(f32[1024,128]{1,0:T(8,128)S(1)} %get-tuple-element.32), channel_id=1, source_target_pairs={{0,1},{1,0},{2,3},{3,2},{4,5},{5,4},{6,7},{7,6},{8,9},{9,8},{10,11... | collective-permute-start | bytes 1572872 | tf_op jit(solution)/shard_map/ppermute | solution.py:225

commit v5 on v4

--- a/solution.py
+++ b/solution.py
@@ -17,6 +17,8 @@
 CHUNK = 40
 N_YZ = 8
 FAR = (0, 4)
+
+NEAR_ORDER = (2, 3, 1)
 
 VMEM = pltpu.VMEM
 F32 = jnp.float32
@@ -247,8 +249,9 @@
     got = lax.all_to_all(
         packed.reshape(DEVICES, 1, 5 * LANES), ("row", "yz", "core"), 0, 0, tiled=True
     )
-    near = call(turn_near, [quarter] * 4)(*far)
-    near = [near[0], *(swap(x, "yz", j) for j, x in enumerate(near) if j)]
+    near = list(call(turn_near, [quarter] * 4)(*far))
+    for j in NEAR_ORDER:
+        near[j] = swap(near[j], "yz", j)
     swapped = call(pack_swapped, (5 * DEVICES, LANES))(slab)
     width = 8 * LANES
     rows, flops = CHIPS * ROWS_OUT, V * V * width

time: 57.1 us -> 57.1 us (level)
  no operation moved by 1% of the time
where the time goes in v5:
time: 57.1 us; the launch traced here: 56.3 us
  starting transfers between devices  21.7 us (38%)
  blocking collectives  17.2 us (30%)
  waiting for transfers between devices  12.4 us (22%)
  Pallas kernels  4.9 us (9%)
    all_to_all x1, blocking collectives, on_device(): lax.all_to_all(share.reshape(CHIPS, ROWS_OUT, LANES), ('row', 'yz'), 0, 0...  17.2 us
    ppermute x6, waiting for transfers between devices, swap(): lax.ppermute(x, axis, [(n, n ^ k) for n in range(lax.axis_size(axis))])  12.4 us
    ppermute x6, starting transfers between devices, swap(): lax.ppermute(x, axis, [(n, n ^ k) for n in range(lax.axis_size(axis))])  11.5 us
    all_to_all x1, starting transfers between devices, on_device(): lax.all_to_all(packed.reshape(DEVICES, 1, 5 * LANES), ('row', 'yz', 'core...  10.2 us
    pallas_call x1, Pallas kernels, on_device(): call(pack_cycle, [half, half, slab.shape], scratch=[VMEM(columns.shape, F...  1.26 us
  transfers between devices with their start and end apart: 7, of which 4 were waited for; matrix products, arithmetic and copies ran while one was open for 0% of the time, Pallas kernels for 4%

profile of v5, /device:TPU:1, one launch (start us, length us, event | category | flops | bytes accessed | tf_op | source)
XLA Modules:
  0.0 56.3 jit_solution(6600251138990989103)
XLA Ops:
  0.0 1.3 %shard_map.28 = (f32[320,128]{1,0:T(8,128)S(1)}, f32[320,128]{1,0:T(8,128)S(1)}, f32[640,128]{1,0:T(8,128)S(1)}) custom-call(f32[32,2560]{1,0:T(8,128)} %bitcast.13, f32[640,128]{1,0:T(8,128)} %bitcast.14), custom_call_target="tpu_custom_call" | custom-call | bytes 1048576 | tf_op jit(solution)/shard_map/pallas_call | solution.py:234
  1.3 1.4 %collective-permute-start = (f32[320,128]{1,0:T(8,128)S(1)}, f32[320,128]{1,0:T(8,128)S(1)}, u32[]{:S(2)}, u32[]{:S(2)}) collective-permute-start(f32[320,128]{1,0:T(8,128)S(1)} %get-tuple-element.23), channel_id=1, source_target_pairs={{0,1},{1,0},{2,3},{3,2},{4,5},{5,4},{6,7},{7,6},{8,9},{9,8},{10,11... | collective-permute-start | bytes 491528 | tf_op jit(solution)/shard_map/ppermute | solution.py:227
  2.7 0.9 %shard_map.29 = f32[640,128]{1,0:T(8,128)} custom-call(f32[640,128]{1,0:T(8,128)S(1)} %get-tuple-element.19.m_ref), custom_call_target="tpu_custom_call" | custom-call | bytes 1048576 | tf_op jit(solution)/shard_map/pallas_call | solution.py:246
  3.7 10.2 %all-to-all-start = ((f32[128,1,640]{2,1,0:T(1,128)}), f32[128,1,640]{2,1,0:T(1,128)S(1)}, u32[]{:S(2)}, u32[]{:S(2)}) async-start(f32[128,1,640]{2,1,0:T(1,128)} %bitcast.4), calls=%async_computation | async-start | bytes 655360 | tf_op jit(solution)/shard_map/all_to_all | solution.py:249
  13.9 0.0 collective-permute-done.other_ref
  13.9 2.9 %collective-permute-start.1 = (f32[320,128]{1,0:T(8,128)S(1)}, f32[320,128]{1,0:T(8,128)S(1)}, u32[]{:S(2)}, u32[]{:S(2)}) collective-permute-start(f32[320,128]{1,0:T(8,128)S(1)} %get-tuple-element.25), channel_id=1, source_target_pairs={{0,8},{2,10},{4,12},{6,14},{8,0},{10,2},{12,4},{14,6},{1,9},{3,11}... | collective-permute-start | bytes 491528 | tf_op jit(solution)/shard_map/ppermute | solution.py:227
  16.9 6.6 %collective-permute-done.1.refs_1_ = f32[320,128]{1,0:T(8,128)S(1)} collective-permute-done((f32[320,128]{1,0:T(8,128)S(1)}, f32[320,128]{1,0:T(8,128)S(1)}, u32[]{:S(2)}, u32[]{:S(2)}) %collective-permute-start.1) | collective-permute-done | bytes 163872 | tf_op jit(solution)/shard_map/ppermute | solution.py:227
  23.5 2.1 %collective-permute-start.2 = (f32[160,128]{1,0:T(8,128)S(1)}, f32[160,128]{1,0:T(8,128)S(1)}, u32[]{:S(2)}, u32[]{:S(2)}) collective-permute-start(f32[160,128]{1,0:T(8,128)S(1)} %get-tuple-element.27), channel_id=1, source_target_pairs={{0,2},{2,0},{4,6},{6,4},{8,10},{10,8},{12,14},{14,12},{1,3},{3,1},... | collective-permute-start | bytes 245768 | tf_op jit(solution)/shard_map/ppermute | solution.py:227
  25.7 3.2 %collective-permute-start.3 = (f32[160,128]{1,0:T(8,128)S(1)}, f32[160,128]{1,0:T(8,128)S(1)}, u32[]{:S(2)}, u32[]{:S(2)}) collective-permute-start(f32[160,128]{1,0:T(8,128)S(1)} %get-tuple-element.28), channel_id=1, source_target_pairs={{0,4},{2,6},{4,0},{6,2},{8,12},{10,14},{12,8},{14,10},{1,5},{3,7},... | collective-permute-start | bytes 245768 | tf_op jit(solution)/shard_map/ppermute | solution.py:227
  28.8 0.0 collective-permute-start.4
  28.8 0.4 shard_map.30.swapped_ref
  29.2 0.0 all-to-all-done
  29.2 0.2 shard_map.31
  29.4 0.0 collective-permute-done.2.w1
  29.4 2.6 %collective-permute-done.3.w2 = f32[160,128]{1,0:T(8,128)S(1)} collective-permute-done((f32[160,128]{1,0:T(8,128)S(1)}, f32[160,128]{1,0:T(8,128)S(1)}, u32[]{:S(2)}, u32[]{:S(2)}) %collective-permute-start.3) | collective-permute-done | bytes 81952 | tf_op jit(solution)/shard_map/ppermute | solution.py:227
  32.0 2.1 %collective-permute-done.4.w3 = f32[160,128]{1,0:T(8,128)S(1)} collective-permute-done((f32[160,128]{1,0:T(8,128)S(1)}, f32[160,128]{1,0:T(8,128)S(1)}, u32[]{:S(2)}, u32[]{:S(2)}) %collective-permute-start.4) | collective-permute-done | bytes 81952 | tf_op jit(solution)/shard_map/ppermute | solution.py:227
  34.2 0.9 %shard_map.34 = (f32[1024,128]{1,0:T(8,128)S(1)}, f32[2,2,256,128]{3,2,1,0:T(8,128)S(1)}, bf16[512,1024]{1,0:T(8,128)(2,1)S(1)}) custom-call(f32[2,2,256,128]{3,2,1,0:T(8,128)S(1)} %get-tuple-element.20.a_core, f32[2,512,128]{2,1,0:T(8,128)S(1)} %get-tuple-element.21.a_row, f32[160,128]{1,0:T(8,128)S(1)} %get-tuple-element.26.w0, ...), custom_call_target="tpu_custom_call" | custom-call | flops 268435456 | bytes 1048576 | tf_op jit(solution)/shard_map/pallas_call | solution.py:263
  35.1 1.8 %collective-permute-start.5 = (f32[1024,128]{1,0:T(8,128)S(1)}, f32[1024,128]{1,0:T(8,128)S(1)}, u32[]{:S(2)}, u32[]{:S(2)}) collective-permute-start(f32[1024,128]{1,0:T(8,128)S(1)} %get-tuple-element.32), channel_id=1, source_target_pairs={{0,1},{1,0},{2,3},{3,2},{4,5},{5,4},{6,7},{7,6},{8,9},{9,8},{10,11... | collective-permute-start | bytes 1572872 | tf_op jit(solution)/shard_map/ppermute | solution.py:227
  36.8 0.6 shard_map.35
  37.4 1.0 %collective-permute-done.5 = f32[1024,128]{1,0:T(8,128)S(1)} collective-permute-done((f32[1024,128]{1,0:T(8,128)S(1)}, f32[1024,128]{1,0:T(8,128)S(1)}, u32[]{:S(2)}, u32[]{:S(2)}) %collective-permute-start.5) | collective-permute-done | bytes 524320 | tf_op jit(solution)/shard_map/ppermute | solution.py:227
  38.4 0.1 add.3
  38.4 17.2 %all_to_all.10 = f32[64,16,128]{2,1,0:T(8,128)S(1)} all-to-all(f32[64,16,128]{2,1,0:T(8,128)S(1)} %bitcast.12), channel_id=1, replica_groups=mesh['row'=8,'yz'=8,'core'=2] {'row','yz'}, dimensions={0} | all-to-all | bytes 1048576 | tf_op jit(solution)/shard_map/all_to_all | solution.py:272
  55.6 0.7 %shard_map.36 = f32[4,512]{1,0:T(4,128)} custom-call(f32[1024,128]{1,0:T(8,128)S(1)} %bitcast.10), custom_call_target="tpu_custom_call" | custom-call | bytes 1048576 | tf_op jit(solution)/shard_map/pallas_call | solution.py:273
  (2 shorter events, 0.1 us)
Async XLA Ops:
  1.3 12.6 %collective-permute-start = (f32[320,128]{1,0:T(8,128)S(1)}, f32[320,128]{1,0:T(8,128)S(1)}, u32[]{:S(2)}, u32[]{:S(2)}) collective-permute-start(f32[320,128]{1,0:T(8,128)S(1)} %get-tuple-element.23), channel_id=1, source_target_pairs={{0,1},{1,0},{2,3},{3,2},{4,5},{5,4},{6,7},{7,6},{8,9},{9,8},{10,11... | collective-permute-start | bytes 491528 | tf_op jit(solution)/shard_map/ppermute | solution.py:227
  3.7 25.6 %all-to-all-start = ((f32[128,1,640]{2,1,0:T(1,128)}), f32[128,1,640]{2,1,0:T(1,128)S(1)}, u32[]{:S(2)}, u32[]{:S(2)}) async-start(f32[128,1,640]{2,1,0:T(1,128)} %bitcast.4), calls=%async_computation | async-start | bytes 655360 | tf_op jit(solution)/shard_map/all_to_all | solution.py:249
  13.9 9.6 %collective-permute-start.1 = (f32[320,128]{1,0:T(8,128)S(1)}, f32[320,128]{1,0:T(8,128)S(1)}, u32[]{:S(2)}, u32[]{:S(2)}) collective-permute-start(f32[320,128]{1,0:T(8,128)S(1)} %get-tuple-element.25), channel_id=1, source_target_pairs={{0,8},{2,10},{4,12},{6,14},{8,0},{10,2},{12,4},{14,6},{1,9},{3,11}... | collective-permute-start | bytes 491528 | tf_op jit(solution)/shard_map/ppermute | solution.py:227
  23.5 5.9 %collective-permute-start.2 = (f32[160,128]{1,0:T(8,128)S(1)}, f32[160,128]{1,0:T(8,128)S(1)}, u32[]{:S(2)}, u32[]{:S(2)}) collective-permute-start(f32[160,128]{1,0:T(8,128)S(1)} %get-tuple-element.27), channel_id=1, source_target_pairs={{0,2},{2,0},{4,6},{6,4},{8,10},{10,8},{12,14},{14,12},{1,3},{3,1},... | collective-permute-start | bytes 245768 | tf_op jit(solution)/shard_map/ppermute | solution.py:227
  25.7 6.4 %collective-permute-start.3 = (f32[160,128]{1,0:T(8,128)S(1)}, f32[160,128]{1,0:T(8,128)S(1)}, u32[]{:S(2)}, u32[]{:S(2)}) collective-permute-start(f32[160,128]{1,0:T(8,128)S(1)} %get-tuple-element.28), channel_id=1, source_target_pairs={{0,4},{2,6},{4,0},{6,2},{8,12},{10,14},{12,8},{14,10},{1,5},{3,7},... | collective-permute-start | bytes 245768 | tf_op jit(solution)/shard_map/ppermute | solution.py:227
  28.8 5.3 %collective-permute-start.4 = (f32[160,128]{1,0:T(8,128)S(1)}, f32[160,128]{1,0:T(8,128)S(1)}, u32[]{:S(2)}, u32[]{:S(2)}) collective-permute-start(f32[160,128]{1,0:T(8,128)S(1)} %get-tuple-element.29), channel_id=1, source_target_pairs={{0,6},{2,4},{4,2},{6,0},{8,14},{10,12},{12,10},{14,8},{1,7},{3,5},... | collective-permute-start | bytes 245768 | tf_op jit(solution)/shard_map/ppermute | solution.py:227
  35.1 3.3 %collective-permute-start.5 = (f32[1024,128]{1,0:T(8,128)S(1)}, f32[1024,128]{1,0:T(8,128)S(1)}, u32[]{:S(2)}, u32[]{:S(2)}) collective-permute-start(f32[1024,128]{1,0:T(8,128)S(1)} %get-tuple-element.32), channel_id=1, source_target_pairs={{0,1},{1,0},{2,3},{3,2},{4,5},{5,4},{6,7},{7,6},{8,9},{9,8},{10,11... | collective-permute-start | bytes 1572872 | tf_op jit(solution)/shard_map/ppermute | solution.py:227
